TPU v7x, 32 devices: a whole 2x2x4 slice. The times are simulated.
32 devices in a mesh: dp: 8 (over y, x, core), tensor: 4 (over z).
Axes of the slice: x: 2, y: 2, z: 4, core: 2. Of those that a mesh axis runs over, the one named last changes fastest.
Arguments:
- tokens: bfloat16 [12608, 512], P(('dp', 'tensor')), may hold values from -11 to 11
- cotangent: bfloat16 [12608, 512], P(('dp', 'tensor')), may hold values from -11 to 11
- routes: int32 [12608, 2], P('dp'), may hold values from 0 to 3, as said below
- slots: int32 [12608, 2], P('dp'), may hold values from -1 to 787, as said below
- norm_gains: bfloat16 [2, 512], P(None, 'dp'), may hold values from 0.5 to 1.5
- norm_biases: bfloat16 [2, 512], P(None, 'dp'), may hold values from -1 to 1
- w_qkv: bfloat16 [3, 512, 512], P(None, 'dp', 'tensor'), may hold values from -0.25 to 0.25
- qv_bias: bfloat16 [2, 512], P(None, ('tensor', 'dp')), may hold values from -1 to 1
- w_out: bfloat16 [512, 512], P('tensor', 'dp'), may hold values from -2 to 2
- out_bias: bfloat16 [512], P('dp'), may hold values from -1 to 1
- w_router: bfloat16 [512, 4], P('dp'), may hold values from -0.25 to 0.25
- w_up: bfloat16 [4, 512, 2048], P(None, 'dp', 'tensor'), may hold values from -0.25 to 0.25
- up_bias: bfloat16 [4, 2048], P(None, ('tensor', 'dp')), may hold values from -1 to 1
- w_down: bfloat16 [4, 2048, 512], P(None, 'tensor', 'dp'), may hold values from -0.5 to 0.5
- down_bias: bfloat16 [4, 512], P(None, 'dp'), may hold values from -1 to 1
Outputs:
- layer_out: float32 [12608, 512], P(('dp', 'tensor'))
- grad_tokens: float32 [12608, 512], P(('dp', 'tensor'))
- grad_norm_gains: float32 [2, 512], P(None, 'dp')
- grad_norm_biases: float32 [2, 512], P(None, 'dp')
- grad_qkv: float32 [3, 512, 512], P(None, 'dp', 'tensor')
- grad_qv_bias: float32 [2, 512], P(None, ('tensor', 'dp'))
- grad_out: float32 [512, 512], P('tensor', 'dp')
- grad_out_bias: float32 [512], P('dp')
- grad_router: float32 [512, 4], P('dp')
- grad_up: float32 [4, 512, 2048], P(None, 'dp', 'tensor')
- grad_up_bias: float32 [4, 2048], P(None, ('tensor', 'dp'))
- grad_down: float32 [4, 2048, 512], P(None, 'tensor', 'dp')
- grad_down_bias: float32 [4, 512], P(None, 'dp')
Inputs may be any that keep to these rules, and one draw needn't show every extreme that they name: `routes`: the two entries of a row name different experts. Within the 1576 rows of one index of dp, the pairs that name an expert take its slots 0, 1, 2, ... in the order of rows and, within a row, of entries; a pair past the first 788 of its expert has -1.
All inputs are finite; a program needn't handle non-finite values.
Results may differ from a plain program's by a relative error of at most 0.025.
Values may be sent and summed in bfloat16 or wider, within the bound.
No kernel may reach another device: no remote copies, remote signals or barrier semaphores. Data moves between devices by JAX's collectives and lax.ppermute only.
A program may use at most 128 MiB of HBM per device.

v0:
```python
from functools import partial

import jax
import jax.numpy as jnp
from jax import lax
from jax.sharding import PartitionSpec as P

HD = 64
EXPERTS = 4
TOP = 2
SEQ = 197
IMG_DEV = 8
CAP = 788


epsilon = 1e-06
precise = lax.Precision.HIGHEST


def norm_forward(values_in, gain_row, bias_row):
    center = values_in - jnp.mean(values_in, axis=-1, keepdims=True)
    inverse = lax.rsqrt(jnp.mean(center * center, axis=-1, keepdims=True) + epsilon)
    normed = center * inverse
    return (normed * gain_row + bias_row, normed, inverse)


def norm_backward(grad_in, normed, inverse, gain_row):
    scaled = grad_in * gain_row
    grad_rows = inverse * (
        scaled
        - jnp.mean(scaled, axis=-1, keepdims=True)
        - normed * jnp.mean(scaled * normed, axis=-1, keepdims=True)
    )
    return (grad_rows, jnp.sum(grad_in * normed, axis=0), jnp.sum(grad_in, axis=0))


def per_device(
    tokens,
    cotangent,
    routes,
    slots,
    norm_gains,
    norm_biases,
    w_qkv,
    qv_bias,
    w_out,
    out_bias,
    w_router,
    w_up,
    up_bias,
    w_down,
    down_bias,
):
    local_rows = tokens.shape[0]
    group_rows = routes.shape[0]
    width = tokens.shape[1]
    tensor_pos = lax.axis_index("tensor")
    full_w = (
        lax.all_gather(norm_gains, "dp", axis=1, tiled=True),
        lax.all_gather(norm_biases, "dp", axis=1, tiled=True),
        lax.all_gather(w_qkv, "dp", axis=1, tiled=True),
        lax.all_gather(qv_bias, "dp", axis=1, tiled=True),
        lax.all_gather(w_out, "dp", axis=1, tiled=True),
        lax.all_gather(out_bias, "dp", axis=0, tiled=True),
        lax.all_gather(w_router, "dp", axis=0, tiled=True),
        lax.all_gather(w_up, "dp", axis=1, tiled=True),
        lax.all_gather(up_bias, "dp", axis=1, tiled=True),
        lax.all_gather(w_down, "dp", axis=2, tiled=True),
        lax.all_gather(down_bias, "dp", axis=1, tiled=True),
    )
    (
        gains_full,
        biases_full,
        qkv_full,
        qvb_full,
        out_full,
        obias_full,
        router_full,
        up_full,
        ubias_full,
        down_full,
        dbias_full,
    ) = full_w
    resid_in = tokens.astype(jnp.float32)
    gain_rows = gains_full.astype(jnp.float32)
    bias_rows = biases_full.astype(jnp.float32)
    normed_one, norm_one, inverse_one = norm_forward(resid_in, gain_rows[0], bias_rows[0])
    first_low = normed_one.astype(jnp.bfloat16)
    first_all = lax.all_gather(first_low, "tensor", axis=0, tiled=True)
    projected = jnp.einsum("td,sdc->stc", first_all, qkv_full, preferred_element_type=jnp.float32)
    qv_rows = qvb_full.astype(jnp.float32)
    local_heads = qkv_full.shape[2] // HD
    shape_four = (IMG_DEV, SEQ, local_heads, HD)
    queries = (projected[0] + qv_rows[0]).astype(jnp.bfloat16).reshape(shape_four)
    key_rows = projected[1].astype(jnp.bfloat16).reshape(shape_four)
    values = (projected[2] + qv_rows[1]).astype(jnp.bfloat16).reshape(shape_four)
    score_scale = HD ** (-0.5)
    scores = (
        jnp.einsum("ishd,ijhd->ihsj", queries, key_rows, preferred_element_type=jnp.float32)
        * score_scale
    )
    log_total = jax.nn.logsumexp(scores, axis=-1, keepdims=True)
    weights_low = jnp.exp(scores - log_total).astype(jnp.bfloat16)
    mixed = jnp.einsum("ihsj,ijhd->ishd", weights_low, values, preferred_element_type=jnp.float32)
    heads_low = mixed.reshape(group_rows, -1).astype(jnp.bfloat16)
    block_rows = heads_low
    attn_core = lax.psum_scatter(
        jnp.dot(block_rows, out_full, preferred_element_type=jnp.float32).astype(jnp.bfloat16),
        "tensor",
        scatter_dimension=0,
        tiled=True,
    ).astype(jnp.float32)
    branch_attn = attn_core + obias_full.astype(jnp.float32)
    resid_mid = resid_in + branch_attn
    normed_two, norm_two, inverse_two = norm_forward(resid_mid, gain_rows[1], bias_rows[1])
    second_low = normed_two.astype(jnp.bfloat16)
    logits = jnp.dot(
        second_low.astype(jnp.float32), router_full.astype(jnp.float32), precision=precise
    )
    probs_all = jax.nn.softmax(logits, axis=-1)
    my_routes = lax.dynamic_slice_in_dim(routes, tensor_pos * local_rows, local_rows, 0)
    my_slots = lax.dynamic_slice_in_dim(slots, tensor_pos * local_rows, local_rows, 0)
    expert_ids = jnp.arange(EXPERTS, dtype=jnp.int32)
    my_choose = (my_routes[:, :, None] == expert_ids).astype(jnp.float32)
    gates_low = jnp.sum(my_choose * probs_all[:, None, :], axis=-1).astype(jnp.bfloat16)
    second_all, gates_all = (
        lax.all_gather(second_low, "tensor", axis=0, tiled=True),
        lax.all_gather(gates_low, "tensor", axis=0, tiled=True),
    )
    target = jnp.where(slots >= 0, routes * CAP + slots, EXPERTS * CAP).reshape(-1)
    spread_rows = jnp.broadcast_to(second_all[:, None, :], (group_rows, TOP, width)).reshape(
        -1, width
    )
    buffer = (
        jnp.zeros((EXPERTS * CAP, width), jnp.bfloat16)
        .at[target]
        .set(spread_rows, mode="drop")
        .reshape(EXPERTS, CAP, width)
    )
    pre_act = (
        jnp.einsum("ecd,edf->ecf", buffer, up_full, preferred_element_type=jnp.float32)
        + ubias_full.astype(jnp.float32)[:, None, :]
    )
    hidden_f, gelu_back = jax.vjp(partial(jax.nn.gelu, approximate=False), pre_act)
    hidden_low = hidden_f.astype(jnp.bfloat16)
    expert_rows = jnp.einsum(
        "ecf,efd->ecd", hidden_low, down_full, preferred_element_type=jnp.float32
    ).reshape(EXPERTS * CAP, width)
    gate_float = gates_all.astype(jnp.float32)
    rows_got = jnp.take(expert_rows, target, axis=0, mode="fill", fill_value=0.0).reshape(
        local_rows * lax.axis_size("tensor"), TOP, width
    )
    moe_part = lax.psum_scatter(
        jnp.sum(gate_float[:, :, None] * rows_got, axis=1).astype(jnp.bfloat16),
        "tensor",
        scatter_dimension=0,
        tiled=True,
    ).astype(jnp.float32)
    kept_local = (my_slots >= 0).astype(jnp.float32)
    gate_local = gates_low.astype(jnp.float32) * kept_local
    bias_mix = jnp.einsum("tk,tke->te", gate_local, my_choose)
    branch_moe = moe_part + jnp.dot(bias_mix, dbias_full.astype(jnp.float32), precision=precise)
    layer_out = resid_mid + branch_moe
    back_w = (
        lax.all_gather(norm_gains, "dp", axis=1, tiled=True),
        lax.all_gather(norm_biases, "dp", axis=1, tiled=True),
        lax.all_gather(w_qkv, "dp", axis=1, tiled=True),
        lax.all_gather(qv_bias, "dp", axis=1, tiled=True),
        lax.all_gather(w_out, "dp", axis=1, tiled=True),
        lax.all_gather(out_bias, "dp", axis=0, tiled=True),
        lax.all_gather(w_router, "dp", axis=0, tiled=True),
        lax.all_gather(w_up, "dp", axis=1, tiled=True),
        lax.all_gather(up_bias, "dp", axis=1, tiled=True),
        lax.all_gather(w_down, "dp", axis=2, tiled=True),
        lax.all_gather(down_bias, "dp", axis=1, tiled=True),
    )
    gains_back = back_w[0].astype(jnp.float32)
    qkv_back = back_w[2]
    out_back = back_w[4]
    router_back = back_w[6].astype(jnp.float32)
    up_back = back_w[7]
    down_back = back_w[9]
    dbias_back = back_w[10].astype(jnp.float32)
    grad_moe = cotangent.astype(jnp.float32)
    cot_all = lax.all_gather(cotangent, "tensor", axis=0, tiled=True)
    cot_float = cot_all.astype(jnp.float32)
    slot_grad = (
        (gate_float[:, :, None] * cot_float[:, None, :]).astype(jnp.bfloat16).reshape(-1, width)
    )
    grad_slots = (
        jnp.zeros((EXPERTS * CAP, width), jnp.bfloat16)
        .at[target]
        .set(slot_grad, mode="drop")
        .reshape(EXPERTS, CAP, width)
    )
    grad_down_bias = jnp.sum(grad_slots, axis=1, dtype=jnp.float32)
    grad_down = jnp.einsum(
        "ecf,ecd->efd", hidden_low, grad_slots, preferred_element_type=jnp.float32
    )
    grad_hidden = jnp.einsum(
        "ecd,efd->ecf", grad_slots, down_back, preferred_element_type=jnp.float32
    )
    grad_pre = gelu_back(grad_hidden)[0].astype(jnp.bfloat16)
    grad_up_bias = jnp.sum(grad_pre, axis=1, dtype=jnp.float32)
    grad_up = jnp.einsum("ecd,ecf->edf", buffer, grad_pre, preferred_element_type=jnp.float32)
    grad_buffer = jnp.einsum(
        "ecf,edf->ecd", grad_pre, up_back, preferred_element_type=jnp.float32
    ).reshape(EXPERTS * CAP, width)
    gathered_in = jnp.take(grad_buffer, target, axis=0, mode="fill", fill_value=0.0).reshape(
        group_rows, TOP, width
    )
    grad_second_part = jnp.sum(gathered_in, axis=1)
    picked_out = jnp.take(expert_rows, target, axis=0, mode="fill", fill_value=0.0).reshape(
        group_rows, TOP, width
    )
    grad_gate_part = jnp.einsum("tkd,td->tk", picked_out, cot_float, precision=precise)
    grad_second_sum, grad_gate_sum = (
        lax.psum_scatter(
            grad_second_part.astype(jnp.bfloat16), "tensor", scatter_dimension=0, tiled=True
        ).astype(jnp.float32),
        lax.psum_scatter(
            grad_gate_part.astype(jnp.bfloat16), "tensor", scatter_dimension=0, tiled=True
        ).astype(jnp.float32),
    )
    bias_inner = jnp.dot(grad_moe, dbias_back.T, precision=precise)
    grad_gates = (grad_gate_sum + jnp.einsum("tke,te->tk", my_choose, bias_inner)) * kept_local
    grad_probs = jnp.einsum("tk,tke->te", grad_gates, my_choose)
    grad_logits = probs_all * (grad_probs - jnp.sum(probs_all * grad_probs, axis=-1, keepdims=True))
    grad_router = jnp.dot(second_low.astype(jnp.float32).T, grad_logits, precision=precise)
    grad_second = grad_second_sum + jnp.dot(grad_logits, router_back.T, precision=precise)
    norm_grad_two, gain_grad_two, bias_grad_two = norm_backward(
        grad_second, norm_two, inverse_two, gains_back[1]
    )
    grad_mid = grad_moe + norm_grad_two
    grad_attn_low = grad_mid.astype(jnp.bfloat16)
    grad_out_bias = jnp.sum(grad_attn_low, axis=0, dtype=jnp.float32)
    grad_attn_all = lax.all_gather(grad_attn_low, "tensor", axis=0, tiled=True)
    grad_out = jnp.dot(heads_low.T, grad_attn_all, preferred_element_type=jnp.float32)
    grad_heads = (
        jnp.dot(grad_attn_all, out_back.T, preferred_element_type=jnp.float32)
        .astype(jnp.bfloat16)
        .reshape(shape_four)
    )
    scores_again = (
        jnp.einsum("ishd,ijhd->ihsj", queries, key_rows, preferred_element_type=jnp.float32)
        * score_scale
    )
    probs_again = jnp.exp(scores_again - log_total)
    grad_weights = jnp.einsum(
        "ishd,ijhd->ihsj", grad_heads, values, preferred_element_type=jnp.float32
    )
    grad_scores = (
        probs_again * (grad_weights - jnp.sum(probs_again * grad_weights, axis=-1, keepdims=True))
    ).astype(jnp.bfloat16)
    grad_values = jnp.einsum(
        "ihsj,ishd->ijhd",
        probs_again.astype(jnp.bfloat16),
        grad_heads,
        preferred_element_type=jnp.float32,
    )
    grad_queries = (
        jnp.einsum("ihsj,ijhd->ishd", grad_scores, key_rows, preferred_element_type=jnp.float32)
        * score_scale
    )
    grad_keys = (
        jnp.einsum("ihsj,ishd->ijhd", grad_scores, queries, preferred_element_type=jnp.float32)
        * score_scale
    )
    grad_proj = (
        jnp.stack([grad_queries, grad_keys, grad_values])
        .reshape(3, group_rows, -1)
        .astype(jnp.bfloat16)
    )
    grad_qv_bias = jnp.stack(
        [
            jnp.sum(grad_proj[0], axis=0, dtype=jnp.float32),
            jnp.sum(grad_proj[2], axis=0, dtype=jnp.float32),
        ]
    )
    grad_qkv = jnp.einsum("td,stc->sdc", first_all, grad_proj, preferred_element_type=jnp.float32)
    block_rows = grad_proj
    grad_first = lax.psum_scatter(
        jnp.einsum("stc,sdc->td", block_rows, qkv_back, preferred_element_type=jnp.float32).astype(
            jnp.bfloat16
        ),
        "tensor",
        scatter_dimension=0,
        tiled=True,
    ).astype(jnp.float32)
    norm_grad_one, gain_grad_one, bias_grad_one = norm_backward(
        grad_first, norm_one, inverse_one, gains_back[0]
    )
    grad_tokens = grad_mid + norm_grad_one
    grad_gains = jnp.stack([gain_grad_one, gain_grad_two])
    grad_biases = jnp.stack([bias_grad_one, bias_grad_two])
    reduced = (
        lax.psum_scatter(grad_gains, "dp", scatter_dimension=1, tiled=True),
        lax.psum_scatter(grad_biases, "dp", scatter_dimension=1, tiled=True),
        lax.psum_scatter(grad_qkv, "dp", scatter_dimension=1, tiled=True),
        lax.psum_scatter(grad_qv_bias, "dp", scatter_dimension=1, tiled=True),
        lax.psum_scatter(grad_out, "dp", scatter_dimension=1, tiled=True),
        lax.psum_scatter(grad_out_bias, "dp", scatter_dimension=0, tiled=True),
        lax.psum_scatter(grad_router, "dp", scatter_dimension=0, tiled=True),
        lax.psum_scatter(grad_up, "dp", scatter_dimension=1, tiled=True),
        lax.psum_scatter(grad_up_bias, "dp", scatter_dimension=1, tiled=True),
        lax.psum_scatter(grad_down, "dp", scatter_dimension=2, tiled=True),
        lax.psum_scatter(grad_down_bias, "dp", scatter_dimension=1, tiled=True),
    )
    gains_sum, biases_sum, obias_sum, router_sum = lax.psum(
        (reduced[0], reduced[1], reduced[5], reduced[6]), "tensor"
    )
    return (
        layer_out,
        grad_tokens,
        gains_sum,
        biases_sum,
        reduced[2],
        reduced[3],
        reduced[4],
        obias_sum,
        router_sum,
        reduced[7],
        reduced[8],
        reduced[9],
        reduced[10],
    )


def solution(mesh):
    placed = (
        P(("dp", "tensor"), None),
        P(("dp", "tensor"), None),
        P("dp", None),
        P("dp", None),
        P(None, "dp"),
        P(None, "dp"),
        P(None, "dp", "tensor"),
        P(None, ("tensor", "dp")),
        P("tensor", "dp"),
        P("dp"),
        P("dp", None),
        P(None, "dp", "tensor"),
        P(None, ("tensor", "dp")),
        P(None, "tensor", "dp"),
        P(None, "dp"),
    )
    return jax.shard_map(
        per_device,
        mesh=mesh,
        in_specs=placed,
        out_specs=(
            P(("dp", "tensor"), None),
            P(("dp", "tensor"), None),
            P(None, "dp"),
            P(None, "dp"),
            P(None, "dp", "tensor"),
            P(None, ("tensor", "dp")),
            P("tensor", "dp"),
            P("dp"),
            P("dp", None),
            P(None, "dp", "tensor"),
            P(None, ("tensor", "dp")),
            P(None, "tensor", "dp"),
            P(None, "dp"),
        ),
        check_vma=False,
    )
```

profile of v0, /device:TPU:0, one launch (start us, length us, event | category | flops | bytes accessed | tf_op | source)
XLA Modules:
  0.0 985.4 jit_solution(676774672855039270)
XLA Ops:
  9.7 10.4 %all-gather = bf16[8,64,2]{1,2,0:T(2,128)(2,1)S(1)} all-gather(bf16[1,64,2]{1,2,0:T(2,128)(2,1)} %bitcast.192), channel_id=1, replica_groups=mesh['dp'=8,'tensor'=4] {'dp'}, dimensions={0}, use_global_device_ids=true | all-gather | bytes 2304 | tf_op jit(solution)/shard_map/all_gather | solution.py:59
  20.2 8.7 all-gather.1
  31.7 8.9 all_gather.58
  40.6 8.5 all-gather.3
  49.4 8.5 all_gather.60
  57.8 11.6 %all-gather.22.cloned.1.call-done = bf16[4,394,512]{2,1,0:T(8,128)(2,1)} async-done(((bf16[1,394,512]{2,1,0:T(8,128)(2,1)}), bf16[4,394,512]{2,1,0:T(8,128)(2,1)}) %all-gather.22.cloned.1.call-update) | async-done | bytes 1613840 | tf_op jit(solution)/shard_map/all_gather | solution.py:89
  80.3 2.8 copy.154
  83.0 2.9 squeeze.4
  89.7 45.1 %fusion = bf16[400,512]{1,0:T(8,128)(2,1)S(1)} fusion(bf16[1576,512]{1,0:T(8,128)(2,1)S(1)} %convolution_convert_fusion), kind=kCustom, calls=%all-reduce-scatter | all-reduce-scatter fusion | flops 819201 | bytes 2023936
  137.7 13.6 %all-reduce = bf16[512]{0:T(512)(128)(2,1)S(1)} all-reduce(bf16[512]{0:T(512)(128)(2,1)S(1)} %dynamic-update-slice), channel_id=1, replica_groups=mesh['dp'=8,'tensor'=4] {'dp'}, use_global_device_ids=true, to_apply=%add | all-reduce | flops 512 | bytes 2048
  157.6 8.0 all-gather.4
  165.7 8.9 all-gather.7
  174.7 8.0 all-gather.8
  186.3 15.2 %mul.228 = f32[1576,2,512]{2,1,0:T(2,128)} broadcast(bf16[1576,512]{1,0:T(8,128)(2,1)S(1)} %reshape.256), dimensions={0,2} | broadcast | bytes 8069120 | tf_op jit(solution)/shard_map/mul | solution.py:188
  201.5 8.7 mul.229
  210.2 2.5 reshape.283
  213.7 11.9 %all-gather.5 = bf16[4,394,2]{1,2,0:T(2,128)(2,1)S(1)} all-gather(bf16[1,394,2]{1,2,0:T(2,128)(2,1)S(1)} %bitcast.176), channel_id=1, replica_groups=mesh['dp'=8,'tensor'=4] {'tensor'}, dimensions={0}, use_global_device_ids=true | all-gather | bytes 7880 | tf_op jit(solution)/shard_map/all_gather | solution.py:128
  226.3 29.5 %scatter_custom_fusion.1 = bf16[3152,512]{1,0:T(8,128)(2,1)} fusion(s32[3152]{0:T(1024)S(1)} %fusion.50, f32[3152,512]{1,0:T(8,128)} %mul.229, f32[3152]{0:T(1024)S(1)} %mul.226, bf16[]{:T(256)} %constant.13.clone.1), kind=kCustom, calls=%fused_computation.34 | custom fusion | flops 3227648 | bytes 9699330 | tf_op jit(solution)/shard_map/scatter | solution.py:193
  255.9 2.2 reshape.196
  258.1 4.2 reshape.250
  262.3 12.9 %broadcast_in_dim.16 = bf16[1576,2,512]{2,1,0:T(2,128)(2,1)} broadcast(bf16[1576,512]{1,0:T(8,128)(2,1)} %reshape.250), dimensions={0,2} | broadcast | bytes 4841472 | tf_op jit(solution)/shard_map/broadcast_in_dim | solution.py:131
  275.2 7.6 reshape.220
  282.9 20.6 %scatter_custom_fusion = bf16[3152,512]{1,0:T(8,128)(2,1)} fusion(s32[3152]{0:T(1024)S(1)} %fusion.50, bf16[3152,512]{1,0:T(8,128)(2,1)} %reshape.220, bf16[]{:T(256)} %constant.13.clone.1), kind=kCustom, calls=%fused_computation.47 | custom fusion | bytes 3228160 | tf_op jit(solution)/shard_map/scatter | solution.py:137
  303.5 3.4 reshape.192
  306.9 10.0 %fusion.15 = (u8[788,512]{1,0:T(8,128)(4,1)}, u8[788,512]{1,0:T(8,128)(4,1)}, f32[4,788,512]{2,1,0:T(8,128)}) fusion(f32[4,512]{1,0:T(4,128)S(1)} %bitcast.162, bf16[4,788,512]{2,1,0:T(8,128)(2,1)} %reshape.192, bf16[4,512,512]{2,1,0:T(8,128)(2,1)} %all-gather.18.cloned.1.call-done), kind=kOutput, calls=%fused_computation.45 | convolution fusion | flops 1674342400 | bytes 12595200 | tf_op jit(solution)/shard_map/ecd,edf->ecf/dot_general | solution.py:141
  316.9 22.0 %convert_reduce_fusion.1 = (f32[4,512]{1,0:T(4,128)S(1)}, bf16[4,788,512]{2,1,0:T(8,128)(2,1)}, f32[4,788,512]{2,1,0:T(8,128)}) fusion(f32[4,788,512]{2,1,0:T(8,128)} %get-tuple-element.126, f32[4,512]{1,0:T(4,128)S(1)} %bitcast.163, u8[788,512]{1,0:T(8,128)(4,1)} %get-tuple-element.80, u8[788,512]{1,0:T(8,128)(4,1)} %get-tuple-element.79, ...), kind=kOutput, calls=%fused_computation.12 | convolution fusion | flops 1781659648 | bytes 22286336 | tf_op jit(solution)/shard_map/ecd,efd->ecf/dot_general | solution.py:200
  338.9 4.8 multiply_convert_fusion
  345.4 4.6 fusion.68
  350.0 5.1 reshape.193
  355.1 6.2 fusion.69
  361.3 5.0 reshape.197
  366.3 13.7 %gather_fusion = f32[3152,512]{1,0:T(8,128)} fusion(f32[3152,512]{1,0:T(8,128)} %reshape.193, s32[4096]{0:T(1024)S(1)} %pad_clamp_fusion), kind=kCustom, calls=%fused_computation.clone | custom fusion | bytes 12923200 | tf_op jit(solution)/shard_map/jit(_take)/gather | solution.py:150
  380.0 13.6 %gather_fusion.1 = f32[3152,512]{1,0:T(8,128)} fusion(f32[3152,512]{1,0:T(8,128)} %reshape.197, s32[4096]{0:T(1024)S(1)} %pad_clamp_fusion), kind=kCustom, calls=%fused_computation.1.clone | custom fusion | bytes 12923200 | tf_op jit(solution)/shard_map/jit(_take)/gather | solution.py:209
  393.6 8.3 broadcast_select_fusion
  401.9 8.3 reshape.198
  410.2 27.0 %reduce_sum.224 = bf16[1576,512]{1,0:T(8,128)(2,1)S(1)} reduce(f32[1576,2,512]{2,1,0:T(2,128)} %reshape.198, f32[]{:T(128)} %constant.50.clone.1), dimensions={1}, to_apply=%region_14.16 | reduce | flops 806912 | bytes 8069124 | tf_op jit(solution)/shard_map/reduce_sum | solution.py:212
  437.3 30.5 %fusion.2 = bf16[400,512]{1,0:T(8,128)(2,1)S(1)} fusion(bf16[1576,512]{1,0:T(8,128)(2,1)S(1)} %reduce_sum.224), kind=kCustom, calls=%all-reduce-scatter.2 | all-reduce-scatter fusion | flops 819201 | bytes 2023936
  469.7 8.3 reshape.195
  478.1 22.5 %fusion.70 = bf16[1576,1,2]{2,1,0:T(2,128)(2,1)S(1)} fusion(f32[1576,2,512]{2,1,0:T(2,128)} %reshape.195, bf16[1576,512,1]{1,2,0:T(2,128)(2,1)} %reshape.283), kind=kOutput, calls=%fused_computation.164 | convolution fusion | flops 19365888 | bytes 8075424 | tf_op jit(solution)/shard_map/tkd,td->tk/dot_general | solution.py:216
  501.6 8.7 all-reduce.4
  516.7 2.4 convert_reduce_fusion
  520.0 12.6 %multiply_reduce_fusion = bf16[1576,512]{1,0:T(8,128)(2,1)} fusion(f32[1576,2,512]{2,1,0:T(2,128)} %reshape.195, f32[1576,2]{1,0:T(8,128)S(1)} %copy.165), kind=kLoop, calls=%fused_computation.28 | loop fusion | flops 2420736 | bytes 8081728 | tf_op jit(solution)/shard_map/reduce_sum | solution.py:154
  535.0 17.9 %all-gather.28.cloned.1.call-done = bf16[4,394,512]{2,1,0:T(8,128)(2,1)} async-done(((bf16[1,394,512]{2,1,0:T(8,128)(2,1)}), bf16[4,394,512]{2,1,0:T(8,128)(2,1)}) %all-gather.28.cloned.1.call-update) | async-done | bytes 1613840 | tf_op jit(solution)/shard_map/all_gather | solution.py:237
  553.0 3.0 reshape.258
  556.0 2.8 convolution_convert_fusion.1
  558.8 2.8 reshape.307
  561.6 3.0 copy.172
  564.6 2.3 multiply_reduce_fusion.1
  580.6 3.4 fusion.12
  584.0 59.7 %fusion.60 = (bf16[400,512]{1,0:T(8,128)(2,1)S(1)}, bf16[400,512]{1,0:T(8,128)(2,1)S(1)}) fusion(bf16[1576,512]{1,0:T(8,128)(2,1)S(1)} %copy-done.21, bf16[1576,512]{1,0:T(8,128)(2,1)} %fusion.12), kind=kCustom, calls=%all-reduce-scatter.4 | all-reduce-scatter fusion | flops 1638401 | bytes 4047360
  650.8 3.8 convolution_bitcast_fusion.2
  654.6 2.4 copy.186
  658.9 7.2 fusion.74
  666.2 7.3 fusion.73
  673.5 4.3 collective-permute-start.1
  682.2 11.8 %all-reduce.7 = f32[512]{0:T(512)S(1)} all-reduce(f32[512]{0:T(512)S(1)} %get-tuple-element.104), channel_id=12, replica_groups=mesh['dp'=8,'tensor'=4] {'dp'}, use_global_device_ids=true, to_apply=%region_38.40.clone | all-reduce | flops 512 | bytes 4096
  694.0 5.0 reduce-scatter.41.cloned.1.call-done
  703.8 31.9 %reduce-scatter.39.cloned.1.call-done = f32[64,2]{1,0:T(8,128)} async-done(((f32[512,2]{1,0:T(8,128)}), f32[64,2]{1,0:T(8,128)}) %reduce-scatter.39.cloned.1.call-update) | async-done | bytes 528
  736.6 35.8 %reduce-scatter.37.cloned.1.call-done = f32[64,2]{1,0:T(8,128)} async-done(((f32[512,2]{1,0:T(8,128)}), f32[64,2]{1,0:T(8,128)}) %reduce-scatter.37.cloned.1.call-update) | async-done | bytes 528
  773.2 12.4 %all-reduce.12 = (f32[2,64]{1,0:T(2,128)}, f32[2,64]{1,0:T(2,128)}, f32[64]{0:T(128)}, f32[64,4]{0,1:T(4,128)}) all-reduce(f32[2,64]{1,0:T(2,128)S(1)} %copy.213, f32[2,64]{1,0:T(2,128)S(1)} %copy.215, f32[64]{0:T(128)S(1)} %dynamic-slice.14, f32[64,4]{0,1:T(4,128)S(1)} %copy.219), channel_id=1, replica_groups=mesh['dp'=8,'tensor'=4] {'tensor'}, use_global_device_ids=true, to_apply=%region_27.29 | all-reduce | flops 576 | bytes 4608 | tf_op jit(solution)/shard_map/psum | solution.py:309
  785.6 46.7 %all-reduce.16.cloned.1.call-done = f32[3,512,128]{2,0,1:T(4,128)} async-done(((f32[3,512,128]{2,0,1:T(4,128)}), f32[3,512,128]{2,0,1:T(4,128)}) %all-reduce.16.cloned.1.call-update) | async-done | bytes 786448
  833.9 34.8 %reduce-scatter.31.cloned.1.call-done = f32[128,64]{0,1:T(8,128)} async-done(((f32[128,512]{0,1:T(8,128)}), f32[128,64]{0,1:T(8,128)}) %reduce-scatter.31.cloned.1.call-update) | async-done | bytes 32784 | tf_op jit(solution)/shard_map/reduce_scatter | solution.py:301
  868.7 55.0 %reduce-scatter.35.cloned.1.call-done = f32[4,512,64]{1,2,0:T(8,128)} async-done(((f32[4,512,512]{1,2,0:T(8,128)}), f32[4,512,64]{1,2,0:T(8,128)}) %reduce-scatter.35.cloned.1.call-update) | async-done | bytes 524304 | tf_op jit(solution)/shard_map/reduce_scatter | solution.py:306
  923.7 55.0 %reduce-scatter.33.cloned.1.call-done = f32[4,64,512]{2,1,0:T(8,128)} async-done(((f32[4,512,512]{2,1,0:T(8,128)}), f32[4,64,512]{2,1,0:T(8,128)}) %reduce-scatter.33.cloned.1.call-update) | async-done | bytes 524304 | tf_op jit(solution)/shard_map/reduce_scatter | solution.py:304
  (334 shorter events, 80.6 us)
Async XLA Ops:
  7.2 62.3 %all-gather.22.cloned.1.call-start = ((), (), s32[]{:S(2)}) async-start(), calls=%async_computation.14 | async-start | bytes 2048000 | tf_op jit(solution)/shard_map/all_gather | solution.py:89
  8.4 49.4 %copy-start.51 = (f32[394]{0:T(512)}, f32[394]{0:T(512)S(1)}, u32[]{:S(2)}) copy-start(f32[394]{0:T(512)S(1)} %broadcast_multiply_fusion.5) | copy-start | bytes 4732
  9.7 48.2 %copy-start.55 = (f32[394]{0:T(512)}, f32[394]{0:T(512)S(1)}, u32[]{:S(2)}) copy-start(f32[394]{0:T(512)S(1)} %add_rsqrt_fusion.1) | copy-start | bytes 4732
  20.2 37.7 %copy-start.57 = (f32[1,512]{1,0:T(1,128)}, f32[1,512]{1,0:T(1,128)S(1)}, u32[]{:S(2)}) copy-start(f32[1,512]{1,0:T(1,128)S(1)} %get-tuple-element.114) | copy-start | bytes 6148
  20.2 133.9 %copy-start.67 = (f32[1,512]{1,0:T(1,128)}, f32[1,512]{1,0:T(1,128)S(1)}, u32[]{:S(2)}) copy-start(f32[1,512]{1,0:T(1,128)S(1)} %get-tuple-element.115) | copy-start | bytes 6148
  30.9 153.5 %all-gather.26.cloned.1.call-start = ((), (), s32[]{:S(2)}) async-start(), calls=%async_computation.16 | async-start | bytes 2048000 | tf_op jit(solution)/shard_map/all_gather | solution.py:185
  31.7 226.5 %all-gather.24.cloned.1.call-start = ((), (), s32[]{:S(2)}) async-start(), calls=%async_computation.15 | async-start | bytes 2048000 | tf_op jit(solution)/shard_map/all_gather | solution.py:127
  40.6 30.7 %copy-start.34 = (bf16[3,512,128]{2,1,0:T(8,128)(2,1)}, bf16[3,512,128]{2,1,0:T(8,128)(2,1)S(1)}, u32[]{:S(2)}) copy-start(bf16[3,512,128]{2,1,0:T(8,128)(2,1)S(1)} %all_gather.58) | copy-start | bytes 1179652
  57.8 31.2 %copy-start.36 = (bf16[128,512]{0,1:T(8,128)(2,1)}, bf16[128,512]{0,1:T(8,128)(2,1)S(1)}, u32[]{:S(2)}) copy-start(bf16[128,512]{0,1:T(8,128)(2,1)S(1)} %all_gather.60) | copy-start | bytes 393220
  88.2 47.9 %copy-start.76 = (u32[32]{0:T(128)S(1)}, u32[32]{0:T(128)}, u32[]{:S(2)}) copy-start(u32[32]{0:T(128)} %constant.121) | copy-start | bytes 388
  88.2 47.9 %copy-start.77 = (u32[32]{0:T(128)S(1)}, u32[32]{0:T(128)}, u32[]{:S(2)}) copy-start(u32[32]{0:T(128)} %constant.133) | copy-start | bytes 388
  88.2 49.2 %copy-start.81 = (bf16[64]{0:T(256)(128)(2,1)S(1)}, bf16[64]{0:T(256)(128)(2,1)}, u32[]{:S(2)}) copy-start(bf16[64]{0:T(256)(128)(2,1)} %param.26) | copy-start | bytes 388
  88.5 64.8 %copy-start.2 = (bf16[394,512]{1,0:T(8,128)(2,1)S(1)}, bf16[394,512]{1,0:T(8,128)(2,1)}, u32[]{:S(2)}) copy-start(bf16[394,512]{1,0:T(8,128)(2,1)} %param.17) | copy-start | bytes 1210372
  89.0 65.0 %copy-start.28 = (bf16[1576,128]{0,1:T(8,128)(2,1)}, bf16[1576,128]{0,1:T(8,128)(2,1)S(1)}, u32[]{:S(2)}) copy-start(bf16[1576,128]{0,1:T(8,128)(2,1)S(1)} %convert_element_type.152) | copy-start | bytes 1210372
  89.7 66.7 %copy-start.63 = (s32[1576,2]{0,1:T(2,128)S(1)}, s32[1576,2]{0,1:T(2,128)}, u32[]{:S(2)}) copy-start(s32[1576,2]{0,1:T(2,128)} %param.19) | copy-start | bytes 37828
  89.7 66.7 %copy-start.64 = (s32[1576,2]{0,1:T(2,128)S(1)}, s32[1576,2]{0,1:T(2,128)}, u32[]{:S(2)}) copy-start(s32[1576,2]{0,1:T(2,128)} %param.20) | copy-start | bytes 37828
  134.8 17.2 %collective-permute-start = (bf16[18,512]{1,0:T(8,128)(2,1)S(1)}, bf16[18,512]{1,0:T(8,128)(2,1)S(1)}, u32[]{:S(2)}, u32[]{:S(2)}) collective-permute-start(bf16[18,512]{1,0:T(8,128)(2,1)S(1)} %slice.52), channel_id=1, source_target_pairs={{0,1},{1,2},{2,3},{4,5},{5,6},{6,7},{8,9},{9,10},{10,11},{12,13},{... | collective-permute-start | bytes 55304
  153.3 30.2 %copy-start.9 = (bf16[418,512]{1,0:T(8,128)(2,1)}, bf16[418,512]{1,0:T(8,128)(2,1)S(1)}, u32[]{:S(2)}) copy-start(bf16[418,512]{1,0:T(8,128)(2,1)S(1)} %concatenate.2) | copy-start | bytes 1284100
  153.3 21.3 %copy-start.80 = (bf16[4,64]{1,0:T(4,128)(2,1)S(1)}, bf16[4,64]{1,0:T(4,128)(2,1)}, u32[]{:S(2)}) copy-start(bf16[4,64]{1,0:T(4,128)(2,1)} %param.31) | copy-start | bytes 1540
  153.3 30.1 %copy-start.30 = (bf16[394,512]{1,0:T(8,128)(2,1)S(1)}, bf16[394,512]{1,0:T(8,128)(2,1)}, u32[]{:S(2)}) copy-start(bf16[394,512]{1,0:T(8,128)(2,1)} %param.18) | copy-start | bytes 1210372
  155.1 151.7 %all-gather.18.cloned.1.call-start = ((), (), s32[]{:S(2)}) async-start(), calls=%async_computation.9 | async-start | bytes 2359296 | tf_op jit(solution)/shard_map/all_gather | solution.py:66
  155.7 161.2 %all-gather.20.cloned.1.call-start = ((), (), s32[]{:S(2)}) async-start(), calls=%async_computation.10 | async-start | bytes 2359296 | tf_op jit(solution)/shard_map/all_gather | solution.py:68
  156.3 396.7 %all-gather.28.cloned.1.call-start = ((), (), s32[]{:S(2)}) async-start(), calls=%async_computation.17 | async-start | bytes 2048000 | tf_op jit(solution)/shard_map/all_gather | solution.py:237
  165.7 47.1 %copy-start.73 = (bf16[512,4]{0,1:T(4,128)(2,1)}, bf16[512,4]{0,1:T(4,128)(2,1)S(1)}, u32[]{:S(2)}) copy-start(bf16[512,4]{0,1:T(4,128)(2,1)S(1)} %reshape.246) | copy-start | bytes 12292
  183.4 29.7 %copy-start.49 = (s32[394,2]{0,1:T(2,128)}, s32[394,2]{0,1:T(2,128)S(1)}, u32[]{:S(2)}) copy-start(s32[394,2]{0,1:T(2,128)S(1)} %constant_dynamic-slice_fusion.1) | copy-start | bytes 9460
  258.1 58.8 %copy-start.12 = (bf16[4,788,512]{2,1,0:T(8,128)(2,1)}, bf16[4,788,512]{2,1,0:T(8,128)(2,1)S(1)}, u32[]{:S(2)}) copy-start(bf16[4,788,512]{2,1,0:T(8,128)(2,1)S(1)} %reshape.196) | copy-start | bytes 9682948
  316.9 22.0 %copy-start.19 = (f32[4,788,512]{2,1,0:T(8,128)S(1)}, f32[4,788,512]{2,1,0:T(8,128)}, u32[]{:S(2)}) copy-start(f32[4,788,512]{2,1,0:T(8,128)} %get-tuple-element.126) | copy-start | bytes 19365892
  467.7 43.4 %collective-permute-start.2 = (bf16[18,512]{1,0:T(8,128)(2,1)S(1)}, bf16[18,512]{1,0:T(8,128)(2,1)S(1)}, u32[]{:S(2)}, u32[]{:S(2)}) collective-permute-start(bf16[18,512]{1,0:T(8,128)(2,1)S(1)} %slice.54), channel_id=1, source_target_pairs={{0,1},{1,2},{2,3},{4,5},{5,6},{6,7},{8,9},{9,10},{10,11},{12,13},{... | collective-permute-start | bytes 55304
  478.0 32.3 %copy-start.70 = (bf16[394,2]{0,1:T(2,128)(2,1)S(1)}, bf16[394,2]{0,1:T(2,128)(2,1)}, u32[]{:S(2)}) copy-start(bf16[394,2]{0,1:T(2,128)(2,1)} %copy-done.69) | copy-start | bytes 4732
  478.0 32.3 %copy-start.75 = (f32[394,2]{0,1:T(2,128)S(1)}, f32[394,2]{0,1:T(2,128)}, u32[]{:S(2)}) copy-start(f32[394,2]{0,1:T(2,128)} %select_reduce_fusion.1) | copy-start | bytes 9460
  478.0 33.1 %copy-start.50 = (s32[394,2]{0,1:T(2,128)S(1)}, s32[394,2]{0,1:T(2,128)}, u32[]{:S(2)}) copy-start(s32[394,2]{0,1:T(2,128)} %copy-done.49) | copy-start | bytes 9460
  478.0 33.1 %copy-start.44 = (f32[394,4]{0,1:T(4,128)S(1)}, f32[394,4]{0,1:T(4,128)}, u32[]{:S(2)}) copy-start(f32[394,4]{0,1:T(4,128)} %copy-done.43) | copy-start | bytes 18916
  478.0 33.1 %copy-start.62 = (f32[394]{0:T(512)S(1)}, f32[394]{0:T(512)}, u32[]{:S(2)}) copy-start(f32[394]{0:T(512)} %copy-done.61) | copy-start | bytes 4732
  478.0 33.1 %copy-start.72 = (f32[394]{0:T(512)S(1)}, f32[394]{0:T(512)}, u32[]{:S(2)}) copy-start(f32[394]{0:T(512)} %copy-done.71) | copy-start | bytes 4732
  478.0 34.6 %copy-start.3 = (bf16[394,512]{1,0:T(8,128)(2,1)S(1)}, bf16[394,512]{1,0:T(8,128)(2,1)}, u32[]{:S(2)}) copy-start(bf16[394,512]{1,0:T(8,128)(2,1)} %param.17) | copy-start | bytes 1210372
  478.0 34.6 %copy-start.10 = (bf16[418,512]{1,0:T(8,128)(2,1)S(1)}, bf16[418,512]{1,0:T(8,128)(2,1)}, u32[]{:S(2)}) copy-start(bf16[418,512]{1,0:T(8,128)(2,1)} %copy-done.9) | copy-start | bytes 1284100
  478.0 34.6 %copy-start.46 = (f32[512]{0:T(512)S(1)}, f32[512]{0:T(512)}, u32[]{:S(2)}) copy-start(f32[512]{0:T(512)} %copy-done.45) | copy-start | bytes 6148
  478.0 34.6 %copy-start.48 = (f32[394,4]{0,1:T(4,128)S(1)}, f32[394,4]{0,1:T(4,128)}, u32[]{:S(2)}) copy-start(f32[394,4]{0,1:T(4,128)} %copy-done.47) | copy-start | bytes 18916
  478.0 34.6 %copy-start.60 = (f32[394]{0:T(512)S(1)}, f32[394]{0:T(512)}, u32[]{:S(2)}) copy-start(f32[394]{0:T(512)} %copy-done.59) | copy-start | bytes 4732
  478.1 34.6 %copy-start.66 = (f32[394]{0:T(512)S(1)}, f32[394]{0:T(512)}, u32[]{:S(2)}) copy-start(f32[394]{0:T(512)} %copy-done.65) | copy-start | bytes 4732
  478.1 34.6 %copy-start.68 = (f32[1,512]{1,0:T(1,128)S(1)}, f32[1,512]{1,0:T(1,128)}, u32[]{:S(2)}) copy-start(f32[1,512]{1,0:T(1,128)} %copy-done.67) | copy-start | bytes 6148
  478.1 34.6 %copy-start.74 = (bf16[512,4]{0,1:T(4,128)(2,1)S(1)}, bf16[512,4]{0,1:T(4,128)(2,1)}, u32[]{:S(2)}) copy-start(bf16[512,4]{0,1:T(4,128)(2,1)} %copy-done.73) | copy-start | bytes 12292
  516.2 162.3 %reduce-scatter.47.cloned.1.call-start = ((), (), s32[]{:S(2)}) async-start(), calls=%async_computation.23 | async-start | bytes 294912
  519.9 160.0 %reduce-scatter.45.cloned.1.call-start = ((), (), s32[]{:S(2)}) async-start(), calls=%async_computation.22 | async-start | bytes 294912
  532.6 23.4 %copy-start.37 = (bf16[128,512]{0,1:T(8,128)(2,1)S(1)}, bf16[128,512]{0,1:T(8,128)(2,1)}, u32[]{:S(2)}) copy-start(bf16[128,512]{0,1:T(8,128)(2,1)} %copy-done.36) | copy-start | bytes 393220
  533.5 147.9 %reduce-scatter.43.cloned.1.call-start = ((), (), s32[]{:S(2)}) async-start(), calls=%async_computation.21 | async-start | bytes 294912
  535.0 29.6 %copy-start.1 = (f32[8,2,197,197]{2,3,1,0:T(8,128)S(1)}, f32[8,2,197,197]{2,3,1,0:T(8,128)}, u32[]{:S(2)}) copy-start(f32[8,2,197,197]{2,3,1,0:T(8,128)} %copy-done) | copy-start | bytes 7451332
  535.0 29.6 %copy-start.39 = (f32[8,2,197]{2,1,0:T(2,128)S(1)}, f32[8,2,197]{2,1,0:T(2,128)}, u32[]{:S(2)}) copy-start(f32[8,2,197]{2,1,0:T(2,128)} %copy-done.38) | copy-start | bytes 37828
  535.0 164.0 %reduce-scatter.41.cloned.1.call-start = ((), (), s32[]{:S(2)}) async-start(), calls=%async_computation.20 | async-start | bytes 73728
  583.9 64.3 %copy-start.4 = (bf16[394,512]{1,0:T(8,128)(2,1)S(1)}, bf16[394,512]{1,0:T(8,128)(2,1)}, u32[]{:S(2)}) copy-start(bf16[394,512]{1,0:T(8,128)(2,1)} %param.17) | copy-start | bytes 1210372
  583.9 64.3 %copy-start.52 = (f32[394]{0:T(512)S(1)}, f32[394]{0:T(512)}, u32[]{:S(2)}) copy-start(f32[394]{0:T(512)} %copy-done.51) | copy-start | bytes 4732
  583.9 64.3 %copy-start.56 = (f32[394]{0:T(512)S(1)}, f32[394]{0:T(512)}, u32[]{:S(2)}) copy-start(f32[394]{0:T(512)} %copy-done.55) | copy-start | bytes 4732
  583.9 64.3 %copy-start.58 = (f32[1,512]{1,0:T(1,128)S(1)}, f32[1,512]{1,0:T(1,128)}, u32[]{:S(2)}) copy-start(f32[1,512]{1,0:T(1,128)} %copy-done.57) | copy-start | bytes 6148
  643.7 3.2 collective-permute-start.3
  646.3 89.5 %reduce-scatter.39.cloned.1.call-start = ((), (), s32[]{:S(2)}) async-start(), calls=%async_computation.19 | async-start | bytes 294912
  649.8 122.6 %reduce-scatter.37.cloned.1.call-start = ((), (), s32[]{:S(2)}) async-start(), calls=%async_computation.18 | async-start | bytes 294912
  650.7 181.5 %all-reduce.16.cloned.1.call-start = ((), (), s32[]{:S(2)}) async-start(), calls=%async_computation.24 | async-start | bytes 2097152
  657.0 211.7 %reduce-scatter.31.cloned.1.call-start = ((), (), s32[]{:S(2)}) async-start(), calls=%async_computation.11 | async-start | bytes 294912 | tf_op jit(solution)/shard_map/reduce_scatter | solution.py:301
  658.6 265.1 %reduce-scatter.35.cloned.1.call-start = ((), (), s32[]{:S(2)}) async-start(), calls=%async_computation.13 | async-start | bytes 4718592 | tf_op jit(solution)/shard_map/reduce_scatter | solution.py:306
  666.1 312.6 %reduce-scatter.33.cloned.1.call-start = ((), (), s32[]{:S(2)}) async-start(), calls=%async_computation.12 | async-start | bytes 4718592 | tf_op jit(solution)/shard_map/reduce_scatter | solution.py:304
  673.4 28.2 %copy-start.11 = (bf16[418,512]{1,0:T(8,128)(2,1)S(1)}, bf16[418,512]{1,0:T(8,128)(2,1)}, u32[]{:S(2)}) copy-start(bf16[418,512]{1,0:T(8,128)(2,1)} %copy-done.9) | copy-start | bytes 1284100
  673.4 28.2 %copy-start.14 = (f32[394,512]{1,0:T(8,128)S(1)}, f32[394,512]{1,0:T(8,128)}, u32[]{:S(2)}) copy-start(f32[394,512]{1,0:T(8,128)} %copy-done.13) | copy-start | bytes 2420740
  673.4 28.2 %copy-start.54 = (bf16[512,4]{0,1:T(4,128)(2,1)S(1)}, bf16[512,4]{0,1:T(4,128)(2,1)}, u32[]{:S(2)}) copy-start(bf16[512,4]{0,1:T(4,128)(2,1)} %copy-done.53) | copy-start | bytes 12292
  673.5 26.9 %collective-permute-start.1 = (bf16[18,512]{1,0:T(8,128)(2,1)S(1)}, bf16[18,512]{1,0:T(8,128)(2,1)S(1)}, u32[]{:S(2)}, u32[]{:S(2)}) collective-permute-start(bf16[18,512]{1,0:T(8,128)(2,1)S(1)} %slice.53), channel_id=1, source_target_pairs={{0,1},{1,2},{2,3},{4,5},{5,6},{6,7},{8,9},{9,10},{10,11},{12,13},{... | collective-permute-start | bytes 55304
  (38 other events, 216.9 us)
Sparse Core Ops, SparseCore 0:
  31.0 38.3 all-gather.21
  71.0 48.7 all-gather.25
  155.3 35.4 all-gather.23
  192.5 26.6 all-gather.17
  220.9 27.7 all-gather.19
  516.3 36.5 all-gather.27
  556.0 32.5 reduce-scatter.46
  591.6 33.6 reduce-scatter.44
  628.3 33.6 reduce-scatter.42
  665.5 33.5 reduce-scatter.40
  702.1 33.6 reduce-scatter.38
  738.7 33.6 reduce-scatter.36
  775.6 56.6 all-reduce.15
  835.7 32.9 reduce-scatter.30
  872.5 51.1 reduce-scatter.34
  927.5 51.1 reduce-scatter.32
where the time goes:
time: 996 us; the launch traced here: 985 us
  waiting for transfers between devices  296 us (30%)
  blocking collectives  263 us (26%)
  local copies, waits for them, and re-layouts  193 us (19%)
  matrix products  106 us (11%)
  other arithmetic  97.8 us (10%)
  between operations  18.2 us (2%)
  starting transfers between devices  10.1 us (1%)
    unnamed x6, blocking collectives  169 us
    unnamed x27, waiting for transfers between devices  122 us
    reduce_scatter x1, waiting for transfers between devices, per_device(): lax.psum_scatter(grad_up, 'dp', scatter_dimension=1, tiled=True)  55 us
    reduce_scatter x1, waiting for transfers between devices, per_device(): lax.psum_scatter(grad_down, 'dp', scatter_dimension=2, tiled=True)  55 us
    unnamed x196, local copies, waits for them, and re-layouts  38.3 us
    reduce_scatter x1, waiting for transfers between devices, per_device(): lax.psum_scatter(grad_out, 'dp', scatter_dimension=1, tiled=True)  34.8 us
    scatter x1, other arithmetic, per_device(): grad_slots = jnp.zeros((EXPERTS * CAP, width), jnp.bfloat16).at[target].s...  29.5 us
    reduce_sum x1, other arithmetic, per_device(): grad_second_part = jnp.sum(gathered_in, axis=1)  27 us
  transfers between devices with their start and end apart: 20, of which 10 were waited for; matrix products, arithmetic and copies ran while one was open for 37% of the time, Pallas kernels for 0%

commit v1 on v0

v1 whole, which is shorter than its diff:
```python
from functools import partial

import jax
import jax.numpy as jnp
from jax import lax
from jax.experimental import pallas as pl
from jax.experimental.pallas import tpu as pltpu
from jax.sharding import PartitionSpec as P

HD = 64
EXPERTS = 4
SEQ = 197
IMG_DEV = 8
CAP = 788
PAD = 200
GROWS = 8
WIN = 224
SLOTROWS = 800
SLOTBUF = (CAP // 16) * 16 + WIN
EPS = 1e-06
BF = jnp.bfloat16
F4 = jnp.float32
NEG = -1e30
LANES = 128

NN = (((1,), (0,)), ((), ()))
NT = (((1,), (1,)), ((), ()))
TN = (((0,), (0,)), ((), ()))

VM = pl.BlockSpec(memory_space=pltpu.VMEM)
SM = pl.BlockSpec(memory_space=pltpu.SMEM)


def mm(a, b, dims=NN):
    return lax.dot_general(a, b, dims, preferred_element_type=F4)


def params():
    return pltpu.CompilerParams(vmem_limit_bytes=60 * 1024 * 1024)


def cost(us):
    return pl.CostEstimate(flops=0, transcendentals=0, bytes_accessed=int(us * 3.3e6))


def xor_send(x, axis, n, mask):
    return lax.ppermute(x, axis, [(i, i ^ mask) for i in range(n)])


def ring_order(n):
    return [0] + list(range(1, n, 2)) + list(range(2, n, 2))[::-1]


def ring_step(x, n, back):
    ring = ring_order(n)
    pairs = [(ring[p], ring[(p + (-1 if back else 1)) % n]) for p in range(n)]
    return lax.ppermute(x, "tensor", pairs)


def ring_sources(n):
    ring = ring_order(n)
    pos = {r: p for p, r in enumerate(ring)}
    return [[ring[(pos[r] - s) % n] for s in range(n)] for r in range(n)]


def stages_of(n):
    if n <= 8:
        inter = list(range(2, n, 2))
        return ([[1]] if n > 1 else []) + ([inter] if inter else [])
    out, bit = [], 1
    while bit < n:
        out.append([bit])
        bit *= 2
    return out


def gather_dp(x, n):
    parts = [((0,), x[None])]
    for stage in reversed(stages_of(n)):
        new = []
        for mask in stage:
            for masks, arr in parts:
                new.append((tuple(k ^ mask for k in masks), xor_send(arr, "dp", n, mask)))
        parts = parts + new
        if n > 8 and stage != [1]:
            parts = [
                (sum((m for m, _ in parts), ()), jnp.concatenate([a for _, a in parts], axis=0))
            ]
    return parts


def scatter_dp(even, odd, n, later):
    got = xor_send(odd, "dp", n, 1)
    masks = list(range(0, n, 2))
    own = {k: even[i] for i, k in enumerate(masks)}
    new = {k: got[i] for i, k in enumerate(masks)}
    own = {k: (own[k].astype(F4) + new[k].astype(F4)).astype(BF) for k in masks}
    stages = stages_of(n)[1:]
    for at, stage in enumerate(stages):
        span = 0
        for m in stage:
            span |= m
        rest = [k for k in masks if not k & span]
        recv = []
        for m in stage:
            pack = [own[k ^ m] for k in rest]
            send = pack[0] if len(pack) == 1 else jnp.stack(pack)
            back = xor_send(send, "dp", n, m)
            recv.append([back] if len(pack) == 1 else [back[i] for i in range(len(pack))])
        masks = rest
        if at == len(stages) - 1:
            return [own[0]] + [r[0] for r in recv]
        own = {
            k: sum((r[i].astype(F4) for r in recv), own[k].astype(F4)).astype(BF)
            for i, k in enumerate(rest)
        }
    return [own[0]]


def add_all(parts):
    return sum((p.astype(F4) for p in parts[1:]), parts[0].astype(F4))


def moments(v, eps_rows):
    center = v - jnp.mean(v, axis=-1, keepdims=True)
    inv = lax.rsqrt(jnp.mean(center * center, axis=-1, keepdims=True) + eps_rows)
    return center * inv, inv


def norm_back(z, normed, inv):
    return inv * (
        z
        - jnp.mean(z, axis=-1, keepdims=True)
        - normed * jnp.mean(z * normed, axis=-1, keepdims=True)
    )


def attn_forward_kernel(masks, width, *refs):
    npieces = len(masks)
    ids = refs[0]
    pieces = refs[1 : 1 + npieces]
    x_ref, rows_ref, router_ref, dbias_ref, slot_ref = refs[1 + npieces : 6 + npieces]
    outs = refs[6 + npieces :]
    if npieces > 0 and masks[0] is not None:
        pay_ref, x1_ref, x1b_ref, q_ref, k_ref, v_ref, o_ref, pb_ref, pr_ref, w_ref = outs
        me, met = ids[0], ids[1]
        for group, ref in zip(masks, pieces):
            dr = ref.shape[3]
            for idx, mask in enumerate(group):
                i = jnp.bitwise_xor(me, mask)
                for jm in range(ref.shape[1]):
                    j = jnp.bitwise_xor(met, jm)
                    for s in range(4):
                        w_ref[
                            s,
                            pl.ds(pl.multiple_of(i * dr, dr), dr),
                            pl.ds(pl.multiple_of(j * LANES, LANES), LANES),
                        ] = ref[idx, jm, s]
    else:
        pay_ref, x1_ref, x1b_ref, q_ref, k_ref, v_ref, o_ref, pb_ref, pr_ref = outs
        w_ref = pieces[0]
    x = x_ref[...].astype(F4)
    n1, _ = moments(x, EPS)
    hn1 = (n1 * rows_ref[0:1, :] + rows_ref[2:3, :]).astype(BF)
    q_ref[...] = (mm(hn1, w_ref[0]) + rows_ref[5:6, :]).astype(BF)
    k_ref[...] = mm(hn1, w_ref[1]).astype(BF)
    v_ref[...] = (mm(hn1, w_ref[2]) + rows_ref[6:7, :]).astype(BF)
    lane = lax.broadcasted_iota(jnp.int32, (PAD, LANES), 1)
    col = lax.broadcasted_iota(jnp.int32, (PAD, PAD), 1)
    for pair in range(width // LANES):
        cols = slice(pair * LANES, (pair + 1) * LANES)
        qp, kp, vp = q_ref[:, cols], k_ref[:, cols], v_ref[:, cols]
        acc = jnp.zeros((PAD, LANES), F4)
        for half in range(2):
            mine = (lane < HD) if half == 0 else (lane >= HD)
            qm = jnp.where(mine, qp * jnp.asarray(HD ** (-0.5), BF), jnp.zeros_like(qp))
            s = mm(qm, kp, NT)
            s = jnp.where(col < SEQ, s, NEG)
            e = jnp.exp(s - jnp.max(s, axis=-1, keepdims=True))
            p = (e * (1.0 / jnp.sum(e, axis=-1, keepdims=True))).astype(BF)
            pb_ref[2 * pair + half] = p
            acc = acc + mm(p, jnp.where(mine, vp, jnp.zeros_like(vp)))
        o_ref[:, cols] = acc.astype(BF)
    x1 = x + (mm(o_ref[...], w_ref[3], NT) + rows_ref[4:5, :])
    x1_ref[...] = x1
    n2, _ = moments(x1, EPS)
    hn2 = (n2 * rows_ref[1:2, :] + rows_ref[3:4, :]).astype(BF)
    logits = mm(router_ref[...], hn2, NT)
    row = lax.broadcasted_iota(jnp.int32, logits.shape, 0)
    logits = jnp.where(row < EXPERTS, logits, NEG)
    e = jnp.exp(logits - jnp.max(logits, axis=0, keepdims=True))
    probs = e / jnp.sum(e, axis=0, keepdims=True)
    pr_ref[...] = probs
    gates = jnp.where(slot_ref[...] >= 0, probs, 0.0).astype(BF)
    pay_ref[0:PAD, :] = hn2
    pay_ref[PAD:, :] = jnp.zeros((GROWS, width), BF)
    pay_ref[PAD:, 0:PAD] = gates
    x1b_ref[...] = x1 + mm(gates, dbias_ref[...], TN)


def attn_forward(ids, weights, x, rows, router, dbias, slot, first):
    width = x.shape[1]
    heads = width // HD
    if first:
        masks = [m for m, _ in weights]
        arrays = [a for _, a in weights]
    else:
        masks, arrays = [None], [weights]
    shapes = [
        jax.ShapeDtypeStruct((PAD + GROWS, width), BF),
        jax.ShapeDtypeStruct((PAD, width), F4),
        jax.ShapeDtypeStruct((PAD, width), F4),
        jax.ShapeDtypeStruct((PAD, width), BF),
        jax.ShapeDtypeStruct((PAD, width), BF),
        jax.ShapeDtypeStruct((PAD, width), BF),
        jax.ShapeDtypeStruct((PAD, width), BF),
        jax.ShapeDtypeStruct((heads, PAD, PAD), BF),
        jax.ShapeDtypeStruct((8, PAD), F4),
    ]
    if first:
        shapes.append(jax.ShapeDtypeStruct((4, width, width), BF))
    return pl.pallas_call(
        partial(attn_forward_kernel, masks, width),
        out_shape=shapes,
        in_specs=[SM] + [VM] * (len(arrays) + 5),
        out_specs=[VM] * len(shapes),
        compiler_params=params(),
        cost_estimate=cost(8),
        name="attn_forward",
    )(ids, *arrays, x, rows, router, dbias, slot)


def one_hot(slot_row, base, rows):
    want = lax.broadcasted_iota(jnp.int32, (rows, slot_row.shape[1]), 0)
    return want == jnp.broadcast_to(slot_row - base, (rows, slot_row.shape[1]))


def dispatch_kernel(nshard, nimg, starts_ref, src_ref, slots_ref, *refs):
    count = nshard * nimg
    pays, cots = refs[:count], refs[count : 2 * count]
    buf_ref, dout_ref = refs[2 * count :]
    buf_ref[...] = jnp.zeros(buf_ref.shape, BF)
    dout_ref[...] = jnp.zeros(dout_ref.shape, BF)
    for s in range(nshard):
        for img in range(nimg):
            pay, cot = pays[s * nimg + img], cots[s * nimg + img]
            tile = src_ref[s] * nimg + img

            def body(e, carry, pay=pay, cot=cot, tile=tile):
                base = pl.multiple_of((starts_ref[tile * EXPERTS + e] // 16) * 16, 16)
                hit = one_hot(slots_ref[tile * EXPERTS + e], base, WIN)
                gate = pay[PAD:, 0:PAD].astype(F4)
                pick = lax.broadcasted_iota(jnp.int32, gate.shape, 0) == e
                gate = jnp.sum(jnp.where(pick, gate, 0.0), axis=0, keepdims=True)
                plain = jnp.where(hit, 1.0, 0.0).astype(BF)
                gated = jnp.where(hit, jnp.broadcast_to(gate, hit.shape), 0.0).astype(BF)
                at = pl.ds(base, WIN)
                buf_ref[e, at, :] = buf_ref[e, at, :] + mm(plain, pay[0:PAD, :]).astype(BF)
                dout_ref[e, at, :] = dout_ref[e, at, :] + mm(gated, cot[...]).astype(BF)
                return carry

            lax.fori_loop(0, EXPERTS, body, 0)


def dispatch(starts, src, slots, pays, cots, nshard, nimg):
    width = pays[0].shape[1]
    shape = jax.ShapeDtypeStruct((EXPERTS, SLOTBUF, width), BF)
    return pl.pallas_call(
        partial(dispatch_kernel, nshard, nimg),
        out_shape=[shape, shape],
        in_specs=[SM, SM] + [VM] * (1 + 2 * len(pays)),
        out_specs=[VM, VM],
        compiler_params=params(),
        cost_estimate=cost(8),
        name="dispatch",
    )(starts, src, slots, *pays, *cots)


def expert_kernel(masks, gmasks, *refs):
    npieces = len(masks)
    ids = refs[0]
    pieces = refs[1 : 1 + npieces]
    ub_ref, buf_ref, dout_ref = refs[1 + npieces : 4 + npieces]
    ngrads = len(gmasks)
    eo_ref, db_ref, gub_ref = refs[4 + npieces : 7 + npieces]
    grads = refs[7 + npieces : 7 + npieces + ngrads]
    up_ref, dn_ref, h_ref, dhp_ref, res_ref = refs[7 + npieces + ngrads :]
    me = ids[0]
    for group, ref in zip(masks, pieces):
        dr = ref.shape[3]
        for idx, mask in enumerate(group):
            at = pl.ds(pl.multiple_of(jnp.bitwise_xor(me, mask) * dr, dr), dr)
            up_ref[at, :] = ref[idx, 0, 0]
            dn_ref[at, :] = ref[idx, 1, 0]
    chunk = SLOTROWS // 2
    gub = jnp.zeros(gub_ref.shape, F4)
    for c in range(2):
        at = slice(c * chunk, (c + 1) * chunk)
        u = mm(buf_ref[at, :], up_ref[...]) + ub_ref[...]
        phi = 0.5 + 0.5 * lax.erf(u * (2.0 ** (-0.5)))
        slope = phi + u * (jnp.exp(-0.5 * u * u) * 0.3989422804014327)
        h_ref[at, :] = (u * phi).astype(BF)
        eo_ref[at, :] = mm(h_ref[at, :], dn_ref[...], NT).astype(BF)
        dh = mm(dout_ref[at, :], dn_ref[...])
        dhp = (dh * slope).astype(BF)
        dhp_ref[at, :] = dhp
        gub = gub + jnp.sum(dhp.astype(F4), axis=0, keepdims=True)
        db_ref[at, :] = mm(dhp, up_ref[...], NT).astype(BF)
    gub_ref[...] = gub
    tail = eo_ref.shape[0] - SLOTROWS
    eo_ref[SLOTROWS:, :] = jnp.zeros((tail, eo_ref.shape[1]), BF)
    db_ref[SLOTROWS:, :] = jnp.zeros((tail, eo_ref.shape[1]), BF)
    for which in range(2):
        if which == 0:
            res_ref[...] = mm(buf_ref[0:SLOTROWS, :], dhp_ref[...], TN)
        else:
            res_ref[...] = mm(dout_ref[0:SLOTROWS, :], h_ref[...], TN)
        for group, ref in zip(gmasks, grads):
            dr = ref.shape[3]
            for idx, mask in enumerate(group):
                at = pl.ds(pl.multiple_of(jnp.bitwise_xor(me, mask) * dr, dr), dr)
                ref[idx, which, 0] = res_ref[at, :].astype(BF)


def experts(ids, weights, ubias, buf, dout, gmasks):
    width = buf.shape[2]
    ff = ubias.shape[2]
    masks = [m for m, _ in weights]
    arrays = [a for _, a in weights]
    dr = arrays[0].shape[3]
    specs = [
        pl.BlockSpec((len(m), 2, 1, dr, ff), lambda e: (0, 0, e, 0, 0)) for m in masks
    ]
    slot_spec = pl.BlockSpec((None, SLOTBUF, width), lambda e: (e, 0, 0))
    row_spec = pl.BlockSpec((None, 1, ff), lambda e: (e, 0, 0))
    gspecs = [
        pl.BlockSpec((len(m), 2, 1, dr, ff), lambda e: (0, 0, e, 0, 0)) for m in gmasks
    ]
    return pl.pallas_call(
        partial(expert_kernel, masks, gmasks),
        grid=(EXPERTS,),
        out_shape=[
            jax.ShapeDtypeStruct((EXPERTS, SLOTBUF, width), BF),
            jax.ShapeDtypeStruct((EXPERTS, SLOTBUF, width), BF),
            jax.ShapeDtypeStruct((EXPERTS, 1, ff), F4),
        ]
        + [jax.ShapeDtypeStruct((len(m), 2, EXPERTS, dr, ff), BF) for m in gmasks],
        in_specs=[SM] + specs + [row_spec, slot_spec, slot_spec],
        out_specs=[slot_spec, slot_spec, row_spec] + gspecs,
        scratch_shapes=[
            pltpu.VMEM((width, ff), BF),
            pltpu.VMEM((width, ff), BF),
            pltpu.VMEM((SLOTROWS, ff), BF),
            pltpu.VMEM((SLOTROWS, ff), BF),
            pltpu.VMEM((width, ff), F4),
        ],
        compiler_params=params(),
        cost_estimate=cost(25),
        name="experts",
    )(ids, *arrays, ubias, buf, dout)


def combine_kernel(nshard, nimg, starts_ref, src_ref, slots_ref, eo_ref, db_ref, *refs):
    count = nshard * nimg
    pays, cots = refs[:count], refs[count : 2 * count]
    m_refs = refs[2 * count : 2 * count + nshard]
    d_refs = refs[2 * count + nshard : 3 * count + nshard]
    s_ref, g_ref, ecat_ref, dcat_ref = refs[3 * count + nshard :]
    width = eo_ref.shape[2]
    for s in range(nshard):
        for img in range(nimg):
            n = s * nimg + img
            pay, cot = pays[n], cots[n]
            tile = src_ref[s] * nimg + img

            def body(e, carry, pay=pay, tile=tile):
                base = pl.multiple_of((starts_ref[tile * EXPERTS + e] // 16) * 16, 16)
                hit = one_hot(slots_ref[tile * EXPERTS + e], base, WIN)
                gate = pay[PAD:, 0:PAD].astype(F4)
                pick = lax.broadcasted_iota(jnp.int32, gate.shape, 0) == e
                gate = jnp.sum(jnp.where(pick, gate, 0.0), axis=0, keepdims=True)
                to = pl.ds(pl.multiple_of(e * WIN, WIN), WIN)
                s_ref[to, :] = jnp.where(hit, 1.0, 0.0).astype(BF)
                g_ref[to, :] = jnp.where(hit, jnp.broadcast_to(gate, hit.shape), 0.0).astype(BF)
                ecat_ref[to, :] = eo_ref[e, pl.ds(base, WIN), :]
                dcat_ref[to, :] = db_ref[e, pl.ds(base, WIN), :]
                return carry

            lax.fori_loop(0, EXPERTS, body, 0)
            m_refs[s][img * PAD : (img + 1) * PAD, :] = mm(
                g_ref[...], ecat_ref[...], TN
            ).astype(BF)
            d_refs[n][0:PAD, :] = mm(s_ref[...], dcat_ref[...], TN).astype(BF)
            cross = mm(ecat_ref[...], cot[...], NT)
            rows = []
            for e in range(EXPERTS):
                at = slice(e * WIN, (e + 1) * WIN)
                rows.append(
                    jnp.sum(cross[at, :] * s_ref[at, :].astype(F4), axis=0, keepdims=True)
                )
            d_refs[n][PAD:, :] = jnp.zeros((GROWS, width), BF)
            d_refs[n][PAD:, 0:PAD] = jnp.concatenate(
                rows + [jnp.zeros((GROWS - EXPERTS, PAD), F4)], axis=0
            ).astype(BF)


def combine(starts, src, slots, eo, db, pays, cots, nshard, nimg):
    width = eo.shape[2]
    count = nshard * nimg
    shapes = [jax.ShapeDtypeStruct((nimg * PAD, width), BF)] * nshard + [
        jax.ShapeDtypeStruct((PAD + GROWS, width), BF)
    ] * count
    return pl.pallas_call(
        partial(combine_kernel, nshard, nimg),
        out_shape=shapes,
        in_specs=[SM, SM] + [VM] * (3 + 2 * count),
        out_specs=[VM] * len(shapes),
        scratch_shapes=[
            pltpu.VMEM((EXPERTS * WIN, PAD), BF),
            pltpu.VMEM((EXPERTS * WIN, PAD), BF),
            pltpu.VMEM((EXPERTS * WIN, width), BF),
            pltpu.VMEM((EXPERTS * WIN, width), BF),
        ],
        compiler_params=params(),
        cost_estimate=cost(10),
        name="combine",
    )(starts, src, slots, eo, db, *pays, *cots)


def attn_backward_kernel(
    recv_ref,
    own_ref,
    x_ref,
    cot_ref,
    x1_ref,
    q_ref,
    k_ref,
    v_ref,
    pb_ref,
    pr_ref,
    slot_ref,
    rows_ref,
    router_ref,
    dbias_ref,
    w_ref,
    gtok_ref,
    da_ref,
    dq_ref,
    dk_ref,
    dv_ref,
    hn1_ref,
    small_ref,
    do_ref,
):
    width = x_ref.shape[1]
    got = recv_ref[...].astype(F4) + own_ref[...].astype(F4)
    cot = cot_ref[...]
    cot_f = cot.astype(F4)
    keep = slot_ref[...] >= 0
    inner = mm(dbias_ref[...], cot, NT)
    dp = jnp.where(keep, got[PAD:, 0:PAD] + inner, 0.0)
    probs = pr_ref[...]
    dl = probs * (dp - jnp.sum(probs * dp, axis=0, keepdims=True))
    dl_low = dl.astype(BF)
    n2, inv2 = moments(x1_ref[...], EPS)
    hn2 = (n2 * rows_ref[1:2, :] + rows_ref[3:4, :]).astype(BF)
    gates = jnp.where(keep, probs, 0.0).astype(BF)
    small_ref[8:16, :] = mm(dl_low, hn2)
    small_ref[16:24, :] = mm(gates, cot)
    dh = got[0:PAD, :] + mm(dl_low, router_ref[...], TN)
    small_ref[1:2, :] = jnp.sum(dh * n2, axis=0, keepdims=True)
    small_ref[3:4, :] = jnp.sum(dh, axis=0, keepdims=True)
    dx1 = cot_f + norm_back(dh * rows_ref[1:2, :], n2, inv2)
    da = dx1.astype(BF)
    da_ref[...] = da
    small_ref[6:7, :] = jnp.sum(da.astype(F4), axis=0, keepdims=True)
    small_ref[7:8, :] = jnp.zeros((1, width), F4)
    do_ref[...] = mm(da, w_ref[3]).astype(BF)
    lane = lax.broadcasted_iota(jnp.int32, (PAD, LANES), 1)
    scale = HD ** (-0.5)
    for pair in range(width // LANES):
        cols = slice(pair * LANES, (pair + 1) * LANES)
        qp, kp, vp, dop = q_ref[:, cols], k_ref[:, cols], v_ref[:, cols], do_ref[:, cols]
        zero = jnp.zeros_like(qp)
        dq = jnp.zeros((PAD, LANES), F4)
        dk = jnp.zeros((PAD, LANES), F4)
        dv = jnp.zeros((PAD, LANES), F4)
        for half in range(2):
            mine = (lane < HD) if half == 0 else (lane >= HD)
            pb = pb_ref[2 * pair + half]
            dom = jnp.where(mine, dop, zero)
            dpb = mm(dom, vp, NT)
            p = pb.astype(F4)
            ds = (p * (dpb - jnp.sum(p * dpb, axis=-1, keepdims=True))).astype(BF)
            dv = dv + mm(pb, dom, TN)
            dq = dq + mm(ds, jnp.where(mine, kp, zero))
            dk = dk + mm(ds, jnp.where(mine, qp, zero), TN)
        dq_ref[:, cols] = (dq * scale).astype(BF)
        dk_ref[:, cols] = (dk * scale).astype(BF)
        dv_ref[:, cols] = dv.astype(BF)
    small_ref[4:5, :] = jnp.sum(dq_ref[...].astype(F4), axis=0, keepdims=True)
    small_ref[5:6, :] = jnp.sum(dv_ref[...].astype(F4), axis=0, keepdims=True)
    dh1 = (
        mm(dq_ref[...], w_ref[0], NT)
        + mm(dk_ref[...], w_ref[1], NT)
        + mm(dv_ref[...], w_ref[2], NT)
    )
    n1, inv1 = moments(x_ref[...].astype(F4), EPS)
    hn1_ref[...] = (n1 * rows_ref[0:1, :] + rows_ref[2:3, :]).astype(BF)
    small_ref[0:1, :] = jnp.sum(dh1 * n1, axis=0, keepdims=True)
    small_ref[2:3, :] = jnp.sum(dh1, axis=0, keepdims=True)
    gtok_ref[...] = dx1 + norm_back(dh1 * rows_ref[0:1, :], n1, inv1)


def attn_backward(recv, own, x, cot, x1, q, k, v, pb, pr, slot, rows, router, dbias, full):
    width = x.shape[1]
    shapes = [
        jax.ShapeDtypeStruct((PAD, width), F4),
        jax.ShapeDtypeStruct((PAD, width), BF),
        jax.ShapeDtypeStruct((PAD, width), BF),
        jax.ShapeDtypeStruct((PAD, width), BF),
        jax.ShapeDtypeStruct((PAD, width), BF),
        jax.ShapeDtypeStruct((PAD, width), BF),
        jax.ShapeDtypeStruct((24, width), F4),
    ]
    return pl.pallas_call(
        attn_backward_kernel,
        out_shape=shapes,
        in_specs=[VM] * 15,
        out_specs=[VM] * len(shapes),
        scratch_shapes=[pltpu.VMEM((PAD, width), BF)],
        compiler_params=params(),
        cost_estimate=cost(10),
        name="attn_backward",
    )(recv, own, x, cot, x1, q, k, v, pb, pr, slot, rows, router, dbias, full)


def weight_grad_kernel(nimg, gmasks, ids, *refs):
    ngrads = len(gmasks)
    groups = [refs[6 * i : 6 * i + 6] for i in range(nimg)]
    grads = refs[6 * nimg : 6 * nimg + ngrads]
    res_ref = refs[6 * nimg + ngrads]
    me, met = ids[0], ids[1]
    for s in range(4):
        total = None
        for hn1, dq, dk, dv, da, o in groups:
            left, right = [(hn1, dq), (hn1, dk), (hn1, dv), (da, o)][s]
            term = mm(left[...], right[...], TN)
            total = term if total is None else total + term
        res_ref[...] = total
        for group, ref in zip(gmasks, grads):
            dr = ref.shape[2] // 4
            for idx, mask in enumerate(group):
                i = jnp.bitwise_xor(me, mask)
                for jm in range(ref.shape[1]):
                    j = jnp.bitwise_xor(met, jm)
                    ref[idx, jm, s * dr : (s + 1) * dr, :] = res_ref[
                        pl.ds(pl.multiple_of(i * dr, dr), dr),
                        pl.ds(pl.multiple_of(j * LANES, LANES), LANES),
                    ].astype(BF)


def weight_grads(ids, operands, gmasks, nt, dr):
    nimg = len(operands)
    width = operands[0][0].shape[1]
    shapes = [jax.ShapeDtypeStruct((len(m), nt, 4 * dr, LANES), BF) for m in gmasks]
    return pl.pallas_call(
        partial(weight_grad_kernel, nimg, gmasks),
        out_shape=shapes,
        in_specs=[SM] + [VM] * (6 * nimg),
        out_specs=[VM] * len(shapes),
        scratch_shapes=[pltpu.VMEM((width, width), F4)],
        compiler_params=params(),
        cost_estimate=cost(5),
        name="weight_grads",
    )(ids, *[a for group in operands for a in group])


def per_device(
    nd,
    nt,
    tokens,
    cotangent,
    routes,
    slots,
    norm_gains,
    norm_biases,
    w_qkv,
    qv_bias,
    w_out,
    out_bias,
    w_router,
    w_up,
    up_bias,
    w_down,
    down_bias,
):
    me = lax.axis_index("dp").astype(jnp.int32)
    met = lax.axis_index("tensor").astype(jnp.int32)
    width = tokens.shape[1]
    dr = w_qkv.shape[1]
    nimg = IMG_DEV // nt
    direct = dr % 16 == 0
    ids = jnp.stack([me if direct else jnp.zeros_like(me), met])
    even, odd = list(range(0, nd, 2)), list(range(1, nd, 2))

    def canonical(parts):
        if direct:
            return parts
        masks = sum((m for m, _ in parts), ())
        arr = jnp.concatenate([a for _, a in parts], axis=0)
        place = [masks.index(k) for k in range(nd)]
        order = jnp.asarray(place, jnp.int32)[jnp.bitwise_xor(jnp.arange(nd), me)]
        arr = jnp.take(arr, order, axis=0)
        lead = arr.ndim - 2
        arr = jnp.moveaxis(arr, 0, lead - 1)
        arr = arr.reshape(arr.shape[: lead - 1] + (nd * dr,) + arr.shape[-1:])
        return [((0,), arr[None])]

    gmasks = [even, odd] if direct else [[0]]

    def halves(grads, lead, rows):
        if direct:
            return grads
        whole = grads[0][0]
        shape = whole.shape[:lead] + (rows, nd, dr) + whole.shape[-1:]
        whole = jnp.moveaxis(whole.reshape(shape), lead + 1, 0)
        whole = whole.reshape((nd,) + grads[0].shape[1 : lead + 1] + (rows * dr, whole.shape[-1]))
        return [
            jnp.take(whole, jnp.bitwise_xor(jnp.asarray(m, jnp.int32), me), axis=0)
            for m in (even, odd)
        ]

    chunk = jnp.concatenate([w_qkv, w_out.T[None]], axis=0)
    chunk_z = jnp.stack([chunk] + [xor_send(chunk, "tensor", nt, m) for m in range(1, nt)])
    small = jnp.concatenate(
        [
            norm_gains.reshape(-1),
            norm_biases.reshape(-1),
            out_bias,
            w_router.T.reshape(-1),
            down_bias.reshape(-1),
            up_bias.reshape(-1),
            qv_bias.reshape(-1),
        ]
    )
    small = lax.all_gather(small, "dp", axis=0)
    rows13 = small[:, : 13 * dr].reshape(nd, 13, dr).transpose(1, 0, 2).reshape(13, nd * dr)
    at = 13 * dr
    fr = up_bias.shape[1]
    ubias = small[:, at : at + EXPERTS * fr].reshape(nd, EXPERTS, fr).transpose(1, 0, 2)
    ubias = ubias.reshape(EXPERTS, 1, nd * fr).astype(F4)
    at += EXPERTS * fr
    qr = qv_bias.shape[1]
    qvb = small[:, at:].reshape(nd, 2, qr).transpose(1, 0, 2).reshape(2, nd * qr)
    qvb = lax.all_gather(qvb, "tensor", axis=1, tiled=True)
    rows = jnp.concatenate(
        [rows13[:5].astype(F4), qvb.astype(F4), jnp.zeros((1, width), F4)], axis=0
    )
    blank = jnp.zeros((EXPERTS, width), BF)
    router = jnp.concatenate([rows13[5:9], blank], axis=0)
    dbias = jnp.concatenate([rows13[9:13], blank], axis=0)
    weights = gather_dp(chunk_z, nd)

    pair_routes = routes.reshape(nt * nimg, 1, SEQ, 2)
    pair_slots = slots.reshape(nt * nimg, 1, SEQ, 2)
    ids4 = jnp.arange(8, dtype=jnp.int32)[None, :, None, None]
    table = jnp.max(jnp.where(pair_routes == ids4, pair_slots, -1), axis=-1)
    counts = jnp.sum((table >= 0).astype(jnp.int32), axis=-1)[:, :EXPERTS]
    tiles = nt * nimg
    before = (jnp.arange(tiles)[:, None] > jnp.arange(tiles)[None, :]).astype(jnp.int32)
    starts = jnp.sum(before[:, :, None] * counts[None], axis=1).reshape(-1)
    table = jnp.pad(table, ((0, 0), (0, 0), (0, PAD - SEQ)), constant_values=-1)
    my_slots = lax.dynamic_slice_in_dim(table, met * nimg, nimg, 0)
    table = table[:, :EXPERTS].reshape(tiles * EXPERTS, 1, PAD)
    src = jnp.asarray(ring_sources(nt), jnp.int32)[met]

    x_img = [
        jnp.pad(tokens[i * SEQ : (i + 1) * SEQ], ((0, PAD - SEQ), (0, 0))) for i in range(nimg)
    ]
    c_img = [
        jnp.pad(cotangent[i * SEQ : (i + 1) * SEQ], ((0, PAD - SEQ), (0, 0))) for i in range(nimg)
    ]
    cots = [list(c_img)]
    for s in range(1, nt):
        cots.append([ring_step(c, nt, False) for c in cots[-1]])
    cots = [c for group in cots for c in group]

    both = jnp.stack([w_up, w_down.transpose(0, 2, 1)])
    expert_weights = canonical(gather_dp(both, nd))

    saved = []
    full = canonical(weights)
    for i in range(nimg):
        res = attn_forward(ids, full, x_img[i], rows, router, dbias, my_slots[i], i == 0)
        if i == 0:
            full = res[-1]
        saved.append(res[:9])
    pays = [[r[0] for r in saved]]
    for s in range(1, nt):
        pays.append([ring_step(p, nt, False) for p in pays[-1]])
    pays = [p for group in pays for p in group]

    buf, dout = dispatch(starts, src, table, pays, cots, nt, nimg)
    res = experts(ids, expert_weights, ubias, buf, dout, gmasks)
    eo, db, gub = res[:3]
    egrads = halves(res[3:], 2, 1)
    res = combine(starts, src, table, eo, db, pays, cots, nt, nimg)
    m_parts, d_parts = res[:nt], res[nt:]

    recv = [d_parts[(nt - 1) * nimg + i] for i in range(nimg)]
    for s in range(nt - 2, -1, -1):
        recv = [ring_step(r, nt, True) for r in recv]
        if s > 0:
            recv = [
                (r.astype(F4) + d_parts[s * nimg + i].astype(F4)).astype(BF)
                for i, r in enumerate(recv)
            ]

    expert_sum = add_all(scatter_dp(egrads[0], egrads[1], nd, None))

    operands, smalls, gtoks = [], None, []
    for i in range(nimg):
        pay, x1, x1b, q, k, v, o, pb, pr = saved[i]
        gtok, da, dq, dk, dv, hn1, sm = attn_backward(
            recv[i],
            d_parts[i],
            x_img[i],
            c_img[i],
            x1,
            q,
            k,
            v,
            pb,
            pr,
            my_slots[i],
            rows,
            router,
            dbias,
            full,
        )
        gtoks.append(gtok[:SEQ])
        operands.append((hn1, dq, dk, dv, da, o))
        smalls = sm if smalls is None else smalls + sm
    grads = weight_grads(ids, operands, gmasks, nt, dr if direct else nd * dr)
    grads = halves(grads, 1, 4)

    gub_rows = jnp.zeros((nt, EXPERTS, gub.shape[2]), F4)
    gub_rows = lax.dynamic_update_slice(gub_rows, gub.reshape(1, EXPERTS, -1), (met, 0, 0))
    flat = jnp.concatenate([smalls, gub_rows.reshape(nt * EXPERTS, -1)], axis=0).astype(BF)

    parts = scatter_dp(grads[0], grads[1], nd, None)
    held = add_all(parts).astype(BF)
    for stage in stages_of(nd):
        flat = add_all([flat] + [xor_send(flat, "dp", nd, m) for m in stage]).astype(BF)
    mine = [held[0]] + [xor_send(held[m], "tensor", nt, m) for m in range(1, nt)]
    mine = add_all(mine)
    flat = add_all([flat] + [xor_send(flat, "tensor", nt, m) for m in range(1, nt)])

    m_got = m_parts[nt - 1]
    m_got, _ = lax.optimization_barrier((m_got, recv[-1]))
    for s in range(nt - 2, -1, -1):
        m_got = ring_step(m_got, nt, True)
        if s > 0:
            m_got = (m_got.astype(F4) + m_parts[s].astype(F4)).astype(BF)
    layer_out = jnp.concatenate(
        [
            saved[i][2][:SEQ]
            + (
                m_got[i * PAD : i * PAD + SEQ].astype(F4)
                + m_parts[0][i * PAD : i * PAD + SEQ].astype(F4)
            )
            for i in range(nimg)
        ],
        axis=0,
    )
    grad_tokens = jnp.concatenate(gtoks, axis=0)

    def dp_cut(lo, hi):
        return lax.dynamic_slice(flat, (lo, me * dr), (hi - lo, dr))

    zero = jnp.zeros_like(me)
    g_qvb = lax.dynamic_slice(flat, (zero + 4, (met * nd + me) * qr), (2, qr))
    g_ub = lax.dynamic_slice(flat, (24 + met * EXPERTS, me * fr), (EXPERTS, fr))
    g_qkv = mine[: 3 * dr].reshape(3, dr, LANES)
    g_out = mine[3 * dr :].T
    g_up = expert_sum[0]
    g_down = expert_sum[1].transpose(0, 2, 1)
    return (
        layer_out,
        grad_tokens,
        dp_cut(0, 2),
        dp_cut(2, 4),
        g_qkv,
        g_qvb,
        g_out,
        dp_cut(6, 7)[0],
        dp_cut(8, 12).T,
        g_up,
        g_ub,
        g_down,
        dp_cut(16, 20),
    )


def solution(mesh):
    nd, nt = mesh.shape["dp"], mesh.shape["tensor"]
    placed = (
        P(("dp", "tensor"), None),
        P(("dp", "tensor"), None),
        P("dp", None),
        P("dp", None),
        P(None, "dp"),
        P(None, "dp"),
        P(None, "dp", "tensor"),
        P(None, ("tensor", "dp")),
        P("tensor", "dp"),
        P("dp"),
        P("dp", None),
        P(None, "dp", "tensor"),
        P(None, ("tensor", "dp")),
        P(None, "tensor", "dp"),
        P(None, "dp"),
    )
    return jax.shard_map(
        partial(per_device, nd, nt),
        mesh=mesh,
        in_specs=placed,
        out_specs=(
            P(("dp", "tensor"), None),
            P(("dp", "tensor"), None),
            P(None, "dp"),
            P(None, "dp"),
            P(None, "dp", "tensor"),
            P(None, ("tensor", "dp")),
            P("tensor", "dp"),
            P("dp"),
            P("dp", None),
            P(None, "dp", "tensor"),
            P(None, ("tensor", "dp")),
            P(None, "tensor", "dp"),
            P(None, "dp"),
        ),
        check_vma=False,
    )
```

time: 996 us -> 290 us (0.29)
  blocking collectives: 263 us -> 30.5 us
  waiting for transfers between devices: 296 us -> 85.8 us
  local copies, waits for them, and re-layouts: 193 us -> 21.8 us
  matrix products: 106 us -> 0 us
  other arithmetic: 97.8 us -> 14 us
  Pallas kernels: 0 us -> 78 us
  starting transfers between devices: 10.1 us -> 57.1 us
  between operations: 18.2 us -> 2.07 us
    unnamed x6 -> x1, blocking collectives: 169 us -> 22.6 us
    reduce_scatter x3 -> x0, waiting for transfers between devices: 145 us -> none  [the longest x1 55 us: per_device(): lax.psum_scatter(grad_up, 'dp', scatter_dimension=1, tiled=True)]
    unnamed x27 -> x0, waiting for transfers between devices: 122 us -> none
    dot_general x23 -> x0, matrix products: 105 us -> none  [the longest x1 22.5 us: per_device(): jnp.einsum('tkd,td->tk', picked_out, cot_float, precision=precise)]
    ppermute x0 -> x56, waiting for transfers between devices: none -> 85.8 us  [the longest x21 53.8 us: ring_step(): return lax.ppermute(x, 'tensor', pairs)]
    pallas_call x0 -> x8, Pallas kernels: none -> 78 us  [the longest x1 17.6 us: combine(): pl.pallas_call(partial(combine_kernel, nshard, nimg), out_shape=shapes, i...]
    all_gather x9 -> x1, blocking collectives: 81.6 us -> 7.91 us  [per_device(): qvb = lax.all_gather(qvb, 'tensor', axis=1, tiled=True)]
    ppermute x0 -> x56, starting transfers between devices: none -> 57.1 us  [the longest x35 34.7 us: xor_send(): return lax.ppermute(x, axis, [(i, i ^ mask) for i in range(n)])]
  transfers between devices with their start and end apart: 20 -> 56, of which waited for: 10 -> 24; matrix products, arithmetic and copies ran while one was open for 37% -> 11% of each run, Pallas kernels for 0% -> 13%
where the time goes in v1:
time: 290 us; the launch traced here: 289 us
  waiting for transfers between devices  85.8 us (30%)
  Pallas kernels  78 us (27%)
  starting transfers between devices  57.1 us (20%)
  blocking collectives  30.5 us (11%)
  local copies, waits for them, and re-layouts  21.8 us (8%)
  other arithmetic  14 us (5%)
    ppermute x21, waiting for transfers between devices, ring_step(): return lax.ppermute(x, 'tensor', pairs)  53.8 us
    ppermute x35, starting transfers between devices, xor_send(): return lax.ppermute(x, axis, [(i, i ^ mask) for i in range(n)])  34.7 us
    ppermute x35, waiting for transfers between devices, xor_send(): return lax.ppermute(x, axis, [(i, i ^ mask) for i in range(n)])  32 us
    unnamed x1, blocking collectives  22.6 us
    ppermute x21, starting transfers between devices, ring_step(): return lax.ppermute(x, 'tensor', pairs)  22.3 us
    pallas_call x1, Pallas kernels, combine(): pl.pallas_call(partial(combine_kernel, nshard, nimg), out_shape=shapes, i...  17.6 us
    pallas_call x1, Pallas kernels, experts(): pl.pallas_call(partial(expert_kernel, masks, gmasks), grid=(EXPERTS,), ou...  16.9 us
    pallas_call x1, Pallas kernels, dispatch(): pl.pallas_call(partial(dispatch_kernel, nshard, nimg), out_shape=[shape,...  14.8 us
  transfers between devices with their start and end apart: 56, of which 24 were waited for; matrix products, arithmetic and copies ran while one was open for 11% of the time, Pallas kernels for 13%

profile of v1, /device:TPU:0, one launch (start us, length us, event | category | flops | bytes accessed | tf_op | source)
XLA Modules:
  0.0 289.2 jit_solution(5117828278985723019)
XLA Ops:
  1.6 3.1 %collective-permute-start = (bf16[4,64,128]{2,1,0:T(8,128)(2,1)S(1)}, bf16[4,64,128]{2,1,0:T(8,128)(2,1)S(1)}, u32[]{:S(2)}, u32[]{:S(2)}) collective-permute-start(bf16[4,64,128]{2,1,0:T(8,128)(2,1)S(1)} %get-tuple-element.144), channel_id=1, source_target_pairs={{0,1},{1,0},{2,3},{3,2},{4,5},{5,4},{6,7},{7,6},{8,9},{9,8},{10,11... | collective-permute-start | bytes 196616 | tf_op jit(solution)/shard_map/ppermute | solution.py:47
  4.7 2.6 collective-permute-start.1
  7.3 1.8 slice_select_fusion
  11.1 3.5 %collective-permute-start.24 = (bf16[200,512]{1,0:T(8,128)(2,1)S(1)}, bf16[200,512]{1,0:T(8,128)(2,1)S(1)}, u32[]{:S(2)}, u32[]{:S(2)}) collective-permute-start(bf16[200,512]{1,0:T(8,128)(2,1)S(1)} %pad.23.refs_9_.cot_ref), channel_id=1, source_target_pairs={{0,1},{1,3},{3,2},{2,0},{4,5},{5,7},{7,6},{6,4},{8,9},{9,11},{11,1... | collective-permute-start | bytes 614408 | tf_op jit(solution)/shard_map/ppermute | solution.py:57
  19.1 1.2 dynamic-slice
  22.0 22.6 %all-reduce.5 = bf16[8960]{0:T(1024)(128)(2,1)S(1)} all-reduce(bf16[8960]{0:T(1024)(128)(2,1)S(1)} %dynamic-update-slice), channel_id=2, replica_groups=mesh['dp'=8,'tensor'=4] {'dp'}, use_global_device_ids=true, to_apply=%add.5 | all-reduce | flops 8960 | bytes 35840
  45.1 1.3 collective-permute-start.4
  46.4 2.1 collective-permute-start.5
  48.9 7.9 %all_gather.11 = bf16[2,512]{1,0:T(2,128)(2,1)S(1)} all-gather(bf16[2,128]{1,0:T(2,128)(2,1)S(1)} %reshape.157), channel_id=1, replica_groups=mesh['dp'=8,'tensor'=4] {'tensor'}, dimensions={1}, use_global_device_ids=true | all-gather | bytes 2560 | tf_op jit(solution)/shard_map/all_gather | solution.py:656
  62.1 1.3 collective-permute-start.11
  64.8 2.1 collective-permute-start.12
  68.1 5.6 %attn_forward.2 = (bf16[208,512]{1,0:T(8,128)(2,1)}, f32[200,512]{1,0:T(8,128)}, f32[200,512]{1,0:T(8,128)}, bf16[200,512]{1,0:T(8,128)(2,1)}, bf16[200,512]{1,0...) custom-call(s32[2]{0:T(128)} %pad_add_fusion.refs_0_.ids, ...), custom_call_target="tpu_custom_call" | custom-call | bytes 26400000 | tf_op jit(solution)/shard_map/attn_forward/pallas_call | solution.py:222
  73.7 5.2 %attn_forward.3 = (bf16[208,512]{1,0:T(8,128)(2,1)}, f32[200,512]{1,0:T(8,128)}, f32[200,512]{1,0:T(8,128)}, bf16[200,512]{1,0:T(8,128)(2,1)}, bf16[200,512]{1,0...) custom-call(s32[2]{0:T(128)} %pad_add_fusion.refs_0_.ids, ...), custom_call_target="tpu_custom_call" | custom-call | bytes 26400000 | tf_op jit(solution)/shard_map/attn_forward/pallas_call | solution.py:222
  79.0 2.9 %collective-permute-start.17 = (bf16[208,512]{1,0:T(8,128)(2,1)S(1)}, bf16[208,512]{1,0:T(8,128)(2,1)S(1)}, u32[]{:S(2)}, u32[]{:S(2)}) collective-permute-start(bf16[208,512]{1,0:T(8,128)(2,1)S(1)} %copy-done.6), channel_id=1, source_target_pairs={{0,1},{1,3},{3,2},{2,0},{4,5},{5,7},{7,6},{6,4},{8,9},{9,11},{11,1... | collective-permute-start | bytes 638984 | tf_op jit(solution)/shard_map/ppermute | solution.py:57
  81.9 1.5 collective-permute-start.27
  83.4 3.6 %collective-permute-done.11.refs_3_ = bf16[1,2,4,64,512]{4,3,2,1,0:T(8,128)(2,1)} collective-permute-done((bf16[1,2,4,64,512]{4,3,2,1,0:T(8,128)(2,1)S(1)}, bf16[1,2,4,64,512]{4,3,2,1,0:T(8,128)(2,1)}, u32[]{:S(2)}, u32[]{:S(2)}) %collective-permute-start.11) | collective-permute-done | bytes 524320 | tf_op jit(solution)/shard_map/ppermute | solution.py:47
  87.0 1.2 collective-permute-done.18.refs_3_
  88.9 3.9 %collective-permute-done.17.refs_2_ = bf16[208,512]{1,0:T(8,128)(2,1)S(1)} collective-permute-done((bf16[208,512]{1,0:T(8,128)(2,1)S(1)}, bf16[208,512]{1,0:T(8,128)(2,1)S(1)}, u32[]{:S(2)}, u32[]{:S(2)}) %collective-permute-start.17) | collective-permute-done | bytes 213024 | tf_op jit(solution)/shard_map/ppermute | solution.py:57
  93.1 4.0 %collective-permute-done.27.refs_14_ = bf16[200,512]{1,0:T(8,128)(2,1)S(1)} collective-permute-done((bf16[200,512]{1,0:T(8,128)(2,1)S(1)}, bf16[200,512]{1,0:T(8,128)(2,1)S(1)}, u32[]{:S(2)}, u32[]{:S(2)}) %collective-permute-start.27) | collective-permute-done | bytes 204832 | tf_op jit(solution)/shard_map/ppermute | solution.py:57
  97.2 4.4 %collective-permute-done.28.refs_15_ = bf16[200,512]{1,0:T(8,128)(2,1)S(1)} collective-permute-done((bf16[200,512]{1,0:T(8,128)(2,1)S(1)}, bf16[200,512]{1,0:T(8,128)(2,1)S(1)}, u32[]{:S(2)}, u32[]{:S(2)}) %collective-permute-start.28) | collective-permute-done | bytes 204832 | tf_op jit(solution)/shard_map/ppermute | solution.py:57
  101.6 4.6 %collective-permute-done.20.refs_5_ = bf16[208,512]{1,0:T(8,128)(2,1)S(1)} collective-permute-done((bf16[208,512]{1,0:T(8,128)(2,1)S(1)}, bf16[208,512]{1,0:T(8,128)(2,1)S(1)}, u32[]{:S(2)}, u32[]{:S(2)}) %collective-permute-start.20) | collective-permute-done | bytes 213024 | tf_op jit(solution)/shard_map/ppermute | solution.py:57
  106.1 2.3 collective-permute-done.19.refs_4_
  108.5 6.7 %collective-permute-done.22.refs_7_ = bf16[208,512]{1,0:T(8,128)(2,1)S(1)} collective-permute-done((bf16[208,512]{1,0:T(8,128)(2,1)S(1)}, bf16[208,512]{1,0:T(8,128)(2,1)S(1)}, u32[]{:S(2)}, u32[]{:S(2)}) %collective-permute-start.22) | collective-permute-done | bytes 213024 | tf_op jit(solution)/shard_map/ppermute | solution.py:57
  116.8 1.2 fusion.18.src_ref
  118.0 4.0 %collective-permute-done.21.refs_6_ = bf16[208,512]{1,0:T(8,128)(2,1)S(1)} collective-permute-done((bf16[208,512]{1,0:T(8,128)(2,1)S(1)}, bf16[208,512]{1,0:T(8,128)(2,1)S(1)}, u32[]{:S(2)}, u32[]{:S(2)}) %collective-permute-start.21) | collective-permute-done | bytes 213024 | tf_op jit(solution)/shard_map/ppermute | solution.py:57
  122.7 14.8 %dispatch.1 = (bf16[4,1008,512]{2,1,0:T(8,128)(2,1)}, bf16[4,1008,512]{2,1,0:T(8,128)(2,1)}) custom-call(s32[32]{0:T(128)} %reshape.158.starts_ref, s32[4]{0:T(128)} %fusion.18.src_ref, s32[32,1,200]{2,1,0:T(1,128)} %reshape.175.slots_ref, bf16[208,512]{1,0:T(8,128)(2,1)} %get-tuple-element.69.refs_0_, bf16[208,512]{1,0:T(8,128)(2,1)} %get-tuple-element.71.refs_1_, ...), custom_call_target="tpu_custom_call" | custom-call | bytes 26400000 | tf_op jit(solution)/shard_map/dispatch/pallas_call | solution.py:268
  137.6 16.9 %experts.1 = (bf16[4,1008,512]{2,1,0:T(8,128)(2,1)}, bf16[4,1008,512]{2,1,0:T(8,128)(2,1)}, f32[4,1,512]{2,1,0:T(1,128)}, bf16[4,2,4,64,512]{4,3,2,1,0:T(8,128)(2,1)}, bf16[4,2,4,64,512]{4,3,2,1,0:T(8,128)(2,1)}) custom-call(s32[2]{0:T(128)} %pad_add_fusion.refs_0_.ids, bf16[1,2,4,64,512]{4,3,2,1,0:T(8,128)(2,1)} %copy-done.2, ...), custom_call_target="tpu_custom_call" | custom-call | bytes 82500000 | tf_op jit(solution)/shard_map/experts/pallas_call | solution.py:339
  154.5 17.6 %combine.1 = (bf16[400,512]{1,0:T(8,128)(2,1)}, bf16[400,512]{1,0:T(8,128)(2,1)}, bf16[400,512]{1,0:T(8,128)(2,1)}, bf16[400,512]{1,0:T(8,128)(2,1)}, bf16[208,5...) custom-call(s32[32]{0:T(128)} %reshape.158.starts_ref, ...), custom_call_target="tpu_custom_call" | custom-call | bytes 33000000 | tf_op jit(solution)/shard_map/combine/pallas_call | solution.py:413
  172.1 2.9 %collective-permute-start.29 = (bf16[208,512]{1,0:T(8,128)(2,1)}, bf16[208,512]{1,0:T(8,128)(2,1)S(1)}, u32[]{:S(2)}, u32[]{:S(2)}) collective-permute-start(bf16[208,512]{1,0:T(8,128)(2,1)} %get-tuple-element.77), channel_id=1, source_target_pairs={{0,2},{1,0},{3,1},{2,3},{4,6},{5,4},{7,5},{6,7},{8,10},{9,8},{11,9... | collective-permute-start | bytes 638984 | tf_op jit(solution)/shard_map/ppermute | solution.py:57
  175.0 4.7 %collective-permute-done.35 = bf16[208,512]{1,0:T(8,128)(2,1)S(1)} collective-permute-done((bf16[208,512]{1,0:T(8,128)(2,1)}, bf16[208,512]{1,0:T(8,128)(2,1)S(1)}, u32[]{:S(2)}, u32[]{:S(2)}) %collective-permute-start.35) | collective-permute-done | bytes 213024 | tf_op jit(solution)/shard_map/ppermute | solution.py:57
  179.7 1.0 add_convert_fusion.11
  181.3 3.0 %collective-permute-done.29 = bf16[208,512]{1,0:T(8,128)(2,1)S(1)} collective-permute-done((bf16[208,512]{1,0:T(8,128)(2,1)}, bf16[208,512]{1,0:T(8,128)(2,1)S(1)}, u32[]{:S(2)}, u32[]{:S(2)}) %collective-permute-start.29) | collective-permute-done | bytes 213024 | tf_op jit(solution)/shard_map/ppermute | solution.py:57
  184.3 1.0 add_convert_fusion.13
  185.8 3.0 %collective-permute-done.36 = bf16[208,512]{1,0:T(8,128)(2,1)S(1)} collective-permute-done((bf16[208,512]{1,0:T(8,128)(2,1)S(1)}, bf16[208,512]{1,0:T(8,128)(2,1)S(1)}, u32[]{:S(2)}, u32[]{:S(2)}) %collective-permute-start.36) | collective-permute-done | bytes 213024 | tf_op jit(solution)/shard_map/ppermute | solution.py:57
  188.9 1.0 add_convert_fusion.10
  190.3 3.1 %collective-permute-done.30 = bf16[208,512]{1,0:T(8,128)(2,1)S(1)} collective-permute-done((bf16[208,512]{1,0:T(8,128)(2,1)S(1)}, bf16[208,512]{1,0:T(8,128)(2,1)S(1)}, u32[]{:S(2)}, u32[]{:S(2)}) %collective-permute-start.30) | collective-permute-done | bytes 213024 | tf_op jit(solution)/shard_map/ppermute | solution.py:57
  194.4 1.4 collective-permute-start.31
  197.1 6.6 %attn_backward.2 = (f32[200,512]{1,0:T(8,128)}, bf16[200,512]{1,0:T(8,128)(2,1)}, bf16[200,512]{1,0:T(8,128)(2,1)}, bf16[200,512]{1,0:T(8,128)(2,1)}, bf16[200,5...) custom-call(bf16[208,512]{1,0:T(8,128)(2,1)} %copy-done.33, ...), custom_call_target="tpu_custom_call" | custom-call | bytes 33000000 | tf_op jit(solution)/shard_map/attn_backward/pallas_call | solution.py:526
  204.4 6.6 %attn_backward.3 = (f32[200,512]{1,0:T(8,128)}, bf16[200,512]{1,0:T(8,128)(2,1)}, bf16[200,512]{1,0:T(8,128)(2,1)}, bf16[200,512]{1,0:T(8,128)(2,1)}, bf16[200,5...) custom-call(bf16[208,512]{1,0:T(8,128)(2,1)} %copy-done.32, ...), custom_call_target="tpu_custom_call" | custom-call | bytes 33000000 | tf_op jit(solution)/shard_map/attn_backward/pallas_call | solution.py:526
  212.4 1.0 collective-permute-start.32
  214.3 1.3 collective-permute-start.40
  215.6 1.4 collective-permute-start.41
  217.0 2.0 pad_maximum_fusion.1
  219.0 4.8 %weight_grads.1 = (bf16[4,4,256,128]{3,2,1,0:T(8,128)(2,1)}, bf16[4,4,256,128]{3,2,1,0:T(8,128)(2,1)}) custom-call(s32[2]{0:T(128)} %pad_add_fusion.refs_0_.ids, bf16[200,512]{1,0:T(8,128)(2,1)} %get-tuple-element.107.refs_0_, bf16[200,512]{1,0:T(8,128)(2,1)} %get-tuple-element.108.refs_1_, bf16[200,512]{1,0:T(8,128)(2,1)} %get-tuple-element.109.refs_2_, ...), custom_call_target="tpu_custom_call" | custom-call | bytes 16500000 | tf_op jit(solution)/shard_map/weight_grads/pallas_call | solution.py:567
  223.9 1.1 collective-permute-start.42
  225.0 1.8 collective-permute-start.43
  226.8 1.6 collective-permute-start.44
  228.5 1.5 collective-permute-start.33
  230.9 2.1 collective-permute-done.44
  234.4 6.1 %collective-permute-done.33 = bf16[400,512]{1,0:T(8,128)(2,1)S(1)} collective-permute-done((bf16[400,512]{1,0:T(8,128)(2,1)S(1)}, bf16[400,512]{1,0:T(8,128)(2,1)S(1)}, u32[]{:S(2)}, u32[]{:S(2)}) %collective-permute-start.33) | collective-permute-done | bytes 409632 | tf_op jit(solution)/shard_map/ppermute | solution.py:57
  240.6 3.5 %collective-permute-start.34 = (bf16[400,512]{1,0:T(8,128)(2,1)S(1)}, bf16[400,512]{1,0:T(8,128)(2,1)S(1)}, u32[]{:S(2)}, u32[]{:S(2)}) collective-permute-start(bf16[400,512]{1,0:T(8,128)(2,1)S(1)} %add_convert_fusion.4), channel_id=1, source_target_pairs={{0,2},{1,0},{3,1},{2,3},{4,6},{5,4},{7,5},{6,7},{8,10},{9,8},{11,9... | collective-permute-start | bytes 1228808 | tf_op jit(solution)/shard_map/ppermute | solution.py:57
  246.5 1.3 collective-permute-start.47
  247.7 1.4 collective-permute-start.48
  249.1 2.4 collective-permute-done.34
  251.7 2.1 collective-permute-done.46
  253.9 3.5 %collective-permute-done.47 = bf16[4,256,128]{2,1,0:T(8,128)(2,1)S(1)} collective-permute-done((bf16[4,256,128]{2,1,0:T(8,128)(2,1)S(1)}, bf16[4,256,128]{2,1,0:T(8,128)(2,1)S(1)}, u32[]{:S(2)}, u32[]{:S(2)}) %collective-permute-start.47) | collective-permute-done | bytes 262176 | tf_op jit(solution)/shard_map/ppermute | solution.py:47
  257.3 1.8 collective-permute-done.48
  259.4 2.4 collective-permute-start.50
  261.8 2.0 collective-permute-start.51
  265.0 1.7 collective-permute-start.54
  266.8 1.2 collective-permute-start.55
  270.2 9.0 %collective-permute-done.53 = bf16[2,4,64,512]{3,2,1,0:T(8,128)(2,1)S(1)} collective-permute-done((bf16[2,4,64,512]{3,2,1,0:T(8,128)(2,1)S(1)}, bf16[2,4,64,512]{3,2,1,0:T(8,128)(2,1)S(1)}, u32[]{:S(2)}, u32[]{:S(2)}) %collective-permute-start.53) | collective-permute-done | bytes 524320 | tf_op jit(solution)/shard_map/ppermute | solution.py:47
  279.2 8.6 %collective-permute-done.54 = bf16[2,4,64,512]{3,2,1,0:T(8,128)(2,1)S(1)} collective-permute-done((bf16[2,4,64,512]{3,2,1,0:T(8,128)(2,1)S(1)}, bf16[2,4,64,512]{3,2,1,0:T(8,128)(2,1)S(1)}, u32[]{:S(2)}, u32[]{:S(2)}) %collective-permute-start.54) | collective-permute-done | bytes 524320 | tf_op jit(solution)/shard_map/ppermute | solution.py:47
  288.2 1.0 slice_bitcast_fusion
  (222 shorter events, 36.3 us)
Async XLA Ops:
  0.6 58.2 %copy-start.23 = (bf16[394,512]{1,0:T(8,128)(2,1)S(1)}, bf16[394,512]{1,0:T(8,128)(2,1)}, u32[]{:S(2)}) copy-start(bf16[394,512]{1,0:T(8,128)(2,1)} %param.16) | copy-start | bytes 1210372
  0.7 58.1 %copy-start.31 = (bf16[4,64,512]{2,1,0:T(8,128)(2,1)S(1)}, bf16[4,64,512]{2,1,0:T(8,128)(2,1)}, u32[]{:S(2)}) copy-start(bf16[4,64,512]{2,1,0:T(8,128)(2,1)} %param.27) | copy-start | bytes 786436
  0.7 58.1 %copy-start.30 = (bf16[4,512,64]{1,2,0:T(8,128)(2,1)S(1)}, bf16[4,512,64]{1,2,0:T(8,128)(2,1)}, u32[]{:S(2)}) copy-start(bf16[4,512,64]{1,2,0:T(8,128)(2,1)} %param.29) | copy-start | bytes 786436
  0.7 58.3 %copy-start.35 = (s32[1576,2]{0,1:T(2,128)S(1)}, s32[1576,2]{0,1:T(2,128)}, u32[]{:S(2)}) copy-start(s32[1576,2]{0,1:T(2,128)} %param.18) | copy-start | bytes 37828
  1.6 57.5 %copy-start.36 = (s32[1576,2]{0,1:T(2,128)S(1)}, s32[1576,2]{0,1:T(2,128)}, u32[]{:S(2)}) copy-start(s32[1576,2]{0,1:T(2,128)} %param.19) | copy-start | bytes 37828
  1.6 43.3 %collective-permute-start = (bf16[4,64,128]{2,1,0:T(8,128)(2,1)S(1)}, bf16[4,64,128]{2,1,0:T(8,128)(2,1)S(1)}, u32[]{:S(2)}, u32[]{:S(2)}) collective-permute-start(bf16[4,64,128]{2,1,0:T(8,128)(2,1)S(1)} %get-tuple-element.144), channel_id=1, source_target_pairs={{0,1},{1,0},{2,3},{3,2},{4,5},{5,4},{6,7},{7,6},{8,9},{9,8},{10,11... | collective-permute-start | bytes 196616 | tf_op jit(solution)/shard_map/ppermute | solution.py:47
  4.7 40.2 %collective-permute-start.1 = (bf16[4,64,128]{2,1,0:T(8,128)(2,1)S(1)}, bf16[4,64,128]{2,1,0:T(8,128)(2,1)S(1)}, u32[]{:S(2)}, u32[]{:S(2)}) collective-permute-start(bf16[4,64,128]{2,1,0:T(8,128)(2,1)S(1)} %get-tuple-element.144), channel_id=1, source_target_pairs={{0,2},{1,3},{2,0},{3,1},{4,6},{5,7},{6,4},{7,5},{8,10},{9,11},{10,... | collective-permute-start | bytes 196616 | tf_op jit(solution)/shard_map/ppermute | solution.py:47
  7.3 37.6 %collective-permute-start.2 = (bf16[4,64,128]{2,1,0:T(8,128)(2,1)S(1)}, bf16[4,64,128]{2,1,0:T(8,128)(2,1)S(1)}, u32[]{:S(2)}, u32[]{:S(2)}) collective-permute-start(bf16[4,64,128]{2,1,0:T(8,128)(2,1)S(1)} %get-tuple-element.144), channel_id=1, source_target_pairs={{0,3},{1,2},{2,1},{3,0},{4,7},{5,6},{6,5},{7,4},{8,11},{9,10},{10,... | collective-permute-start | bytes 196616 | tf_op jit(solution)/shard_map/ppermute | solution.py:47
  9.1 64.5 %copy-start.1 = (bf16[200,512]{1,0:T(8,128)(2,1)}, bf16[200,512]{1,0:T(8,128)(2,1)S(1)}, u32[]{:S(2)}) copy-start(bf16[200,512]{1,0:T(8,128)(2,1)S(1)} %get-tuple-element.147.refs_8_.cot_ref) | copy-start | bytes 614404
  9.1 47.7 %collective-permute-start.23 = (bf16[200,512]{1,0:T(8,128)(2,1)S(1)}, bf16[200,512]{1,0:T(8,128)(2,1)S(1)}, u32[]{:S(2)}, u32[]{:S(2)}) collective-permute-start(bf16[200,512]{1,0:T(8,128)(2,1)S(1)} %get-tuple-element.147.refs_8_.cot_ref), channel_id=1, source_target_pairs={{0,1},{1,3},{3,2},{2,0},{4,5},{5,7},{7,6},{6,4},{8,9},{9,11},{11,1... | collective-permute-start | bytes 614408 | tf_op jit(solution)/shard_map/ppermute | solution.py:57
  11.1 62.6 %copy-start = (bf16[200,512]{1,0:T(8,128)(2,1)}, bf16[200,512]{1,0:T(8,128)(2,1)S(1)}, u32[]{:S(2)}) copy-start(bf16[200,512]{1,0:T(8,128)(2,1)S(1)} %pad.23.refs_9_.cot_ref) | copy-start | bytes 614404
  11.1 50.2 %collective-permute-start.24 = (bf16[200,512]{1,0:T(8,128)(2,1)S(1)}, bf16[200,512]{1,0:T(8,128)(2,1)S(1)}, u32[]{:S(2)}, u32[]{:S(2)}) collective-permute-start(bf16[200,512]{1,0:T(8,128)(2,1)S(1)} %pad.23.refs_9_.cot_ref), channel_id=1, source_target_pairs={{0,1},{1,3},{3,2},{2,0},{4,5},{5,7},{7,6},{6,4},{8,9},{9,11},{11,1... | collective-permute-start | bytes 614408 | tf_op jit(solution)/shard_map/ppermute | solution.py:57
  45.0 11.9 %collective-permute-start.3 = (bf16[1,4,4,64,128]{4,3,2,1,0:T(8,128)(2,1)S(1)}, bf16[1,4,4,64,128]{4,3,2,1,0:T(8,128)(2,1)S(1)}, u32[]{:S(2)}, u32[]{:S(2)}) collective-permute-start(bf16[1,4,4,64,128]{4,3,2,1,0:T(8,128)(2,1)S(1)} %maximum_bitcast_fusion.1.refs_1_), channel_id=1, source_target_pairs={{0,8},{4,12},{8,0},{12,4},{16,24},{20,28},{24,16},{28,20},{1,9},{5... | collective-permute-start | bytes 786440 | tf_op jit(solution)/shard_map/ppermute | solution.py:47
  45.1 13.2 %collective-permute-start.4 = (bf16[1,4,4,64,128]{4,3,2,1,0:T(8,128)(2,1)S(1)}, bf16[1,4,4,64,128]{4,3,2,1,0:T(8,128)(2,1)S(1)}, u32[]{:S(2)}, u32[]{:S(2)}) collective-permute-start(bf16[1,4,4,64,128]{4,3,2,1,0:T(8,128)(2,1)S(1)} %maximum_bitcast_fusion.1.refs_1_), channel_id=1, source_target_pairs={{0,16},{4,20},{8,24},{12,28},{16,0},{20,4},{24,8},{28,12},{1,17},{... | collective-permute-start | bytes 786440 | tf_op jit(solution)/shard_map/ppermute | solution.py:47
  46.4 11.9 %collective-permute-start.5 = (bf16[1,4,4,64,128]{4,3,2,1,0:T(8,128)(2,1)S(1)}, bf16[1,4,4,64,128]{4,3,2,1,0:T(8,128)(2,1)S(1)}, u32[]{:S(2)}, u32[]{:S(2)}) collective-permute-start(bf16[1,4,4,64,128]{4,3,2,1,0:T(8,128)(2,1)S(1)} %maximum_bitcast_fusion.1.refs_1_), channel_id=1, source_target_pairs={{0,24},{4,28},{8,16},{12,20},{16,8},{20,12},{24,0},{28,4},{1,25},{... | collective-permute-start | bytes 786440 | tf_op jit(solution)/shard_map/ppermute | solution.py:47
  56.9 5.2 %collective-permute-start.6 = (bf16[1,4,4,64,128]{4,3,2,1,0:T(8,128)(2,1)S(1)}, bf16[1,4,4,64,128]{4,3,2,1,0:T(8,128)(2,1)}, u32[]{:S(2)}, u32[]{:S(2)}) collective-permute-start(bf16[1,4,4,64,128]{4,3,2,1,0:T(8,128)(2,1)S(1)} %maximum_bitcast_fusion.1.refs_1_), channel_id=1, source_target_pairs={{0,4},{4,0},{8,12},{12,8},{16,20},{20,16},{24,28},{28,24},{1,5},{5... | collective-permute-start | bytes 786440 | tf_op jit(solution)/shard_map/ppermute | solution.py:47
  56.9 6.4 %collective-permute-start.7 = (bf16[1,4,4,64,128]{4,3,2,1,0:T(8,128)(2,1)S(1)}, bf16[1,4,4,64,128]{4,3,2,1,0:T(8,128)(2,1)}, u32[]{:S(2)}, u32[]{:S(2)}) collective-permute-start(bf16[1,4,4,64,128]{4,3,2,1,0:T(8,128)(2,1)S(1)} %collective-permute-done.3.refs_2_), channel_id=1, source_target_pairs={{0,4},{4,0},{8,12},{12,8},{16,20},{20,16},{24,28},{28,24},{1,5},{5... | collective-permute-start | bytes 786440 | tf_op jit(solution)/shard_map/ppermute | solution.py:47
  58.3 6.5 %collective-permute-start.8 = (bf16[1,4,4,64,128]{4,3,2,1,0:T(8,128)(2,1)S(1)}, bf16[1,4,4,64,128]{4,3,2,1,0:T(8,128)(2,1)}, u32[]{:S(2)}, u32[]{:S(2)}) collective-permute-start(bf16[1,4,4,64,128]{4,3,2,1,0:T(8,128)(2,1)S(1)} %collective-permute-done.4.refs_3_), channel_id=1, source_target_pairs={{0,4},{4,0},{8,12},{12,8},{16,20},{20,16},{24,28},{28,24},{1,5},{5... | collective-permute-start | bytes 786440 | tf_op jit(solution)/shard_map/ppermute | solution.py:47
  58.3 8.6 %collective-permute-start.9 = (bf16[1,4,4,64,128]{4,3,2,1,0:T(8,128)(2,1)S(1)}, bf16[1,4,4,64,128]{4,3,2,1,0:T(8,128)(2,1)}, u32[]{:S(2)}, u32[]{:S(2)}) collective-permute-start(bf16[1,4,4,64,128]{4,3,2,1,0:T(8,128)(2,1)S(1)} %collective-permute-done.5.refs_4_), channel_id=1, source_target_pairs={{0,4},{4,0},{8,12},{12,8},{16,20},{20,16},{24,28},{28,24},{1,5},{5... | collective-permute-start | bytes 786440 | tf_op jit(solution)/shard_map/ppermute | solution.py:47
  61.3 20.7 %collective-permute-start.10 = (bf16[1,2,4,64,512]{4,3,2,1,0:T(8,128)(2,1)S(1)}, bf16[1,2,4,64,512]{4,3,2,1,0:T(8,128)(2,1)S(1)}, u32[]{:S(2)}, u32[]{:S(2)}) collective-permute-start(bf16[1,2,4,64,512]{4,3,2,1,0:T(8,128)(2,1)S(1)} %maximum_bitcast_fusion.refs_1_), channel_id=1, source_target_pairs={{0,8},{4,12},{8,0},{12,4},{16,24},{20,28},{24,16},{28,20},{1,9},{5... | collective-permute-start | bytes 1572872 | tf_op jit(solution)/shard_map/ppermute | solution.py:47
  62.1 25.0 %collective-permute-start.11 = (bf16[1,2,4,64,512]{4,3,2,1,0:T(8,128)(2,1)S(1)}, bf16[1,2,4,64,512]{4,3,2,1,0:T(8,128)(2,1)}, u32[]{:S(2)}, u32[]{:S(2)}) collective-permute-start(bf16[1,2,4,64,512]{4,3,2,1,0:T(8,128)(2,1)S(1)} %maximum_bitcast_fusion.refs_1_), channel_id=1, source_target_pairs={{0,16},{4,20},{8,24},{12,28},{16,0},{20,4},{24,8},{28,12},{1,17},{... | collective-permute-start | bytes 1572872 | tf_op jit(solution)/shard_map/ppermute | solution.py:47
  63.4 15.5 %collective-permute-start.25 = (bf16[200,512]{1,0:T(8,128)(2,1)S(1)}, bf16[200,512]{1,0:T(8,128)(2,1)S(1)}, u32[]{:S(2)}, u32[]{:S(2)}) collective-permute-start(bf16[200,512]{1,0:T(8,128)(2,1)S(1)} %collective-permute-done.23.refs_10_), channel_id=1, source_target_pairs={{0,1},{1,3},{3,2},{2,0},{4,5},{5,7},{7,6},{6,4},{8,9},{9,11},{11,1... | collective-permute-start | bytes 614408 | tf_op jit(solution)/shard_map/ppermute | solution.py:57
  64.8 28.3 %collective-permute-start.12 = (bf16[1,2,4,64,512]{4,3,2,1,0:T(8,128)(2,1)S(1)}, bf16[1,2,4,64,512]{4,3,2,1,0:T(8,128)(2,1)}, u32[]{:S(2)}, u32[]{:S(2)}) collective-permute-start(bf16[1,2,4,64,512]{4,3,2,1,0:T(8,128)(2,1)S(1)} %maximum_bitcast_fusion.refs_1_), channel_id=1, source_target_pairs={{0,24},{4,28},{8,16},{12,20},{16,8},{20,12},{24,0},{28,4},{1,25},{... | collective-permute-start | bytes 1572872 | tf_op jit(solution)/shard_map/ppermute | solution.py:47
  66.9 12.1 %collective-permute-start.26 = (bf16[200,512]{1,0:T(8,128)(2,1)S(1)}, bf16[200,512]{1,0:T(8,128)(2,1)S(1)}, u32[]{:S(2)}, u32[]{:S(2)}) collective-permute-start(bf16[200,512]{1,0:T(8,128)(2,1)S(1)} %collective-permute-done.24.refs_11_), channel_id=1, source_target_pairs={{0,1},{1,3},{3,2},{2,0},{4,5},{5,7},{7,6},{6,4},{8,9},{9,11},{11,1... | collective-permute-start | bytes 614408 | tf_op jit(solution)/shard_map/ppermute | solution.py:57
  78.9 9.3 %collective-permute-start.18 = (bf16[208,512]{1,0:T(8,128)(2,1)}, bf16[208,512]{1,0:T(8,128)(2,1)S(1)}, u32[]{:S(2)}, u32[]{:S(2)}) collective-permute-start(bf16[208,512]{1,0:T(8,128)(2,1)} %get-tuple-element.71.refs_1_), channel_id=1, source_target_pairs={{0,1},{1,3},{3,2},{2,0},{4,5},{5,7},{7,6},{6,4},{8,9},{9,11},{11,1... | collective-permute-start | bytes 638984 | tf_op jit(solution)/shard_map/ppermute | solution.py:57
  79.0 13.8 %collective-permute-start.17 = (bf16[208,512]{1,0:T(8,128)(2,1)S(1)}, bf16[208,512]{1,0:T(8,128)(2,1)S(1)}, u32[]{:S(2)}, u32[]{:S(2)}) collective-permute-start(bf16[208,512]{1,0:T(8,128)(2,1)S(1)} %copy-done.6), channel_id=1, source_target_pairs={{0,1},{1,3},{3,2},{2,0},{4,5},{5,7},{7,6},{6,4},{8,9},{9,11},{11,1... | collective-permute-start | bytes 638984 | tf_op jit(solution)/shard_map/ppermute | solution.py:57
  81.9 55.6 %copy-start.19 = (bf16[1,2,4,64,512]{4,3,2,1,0:T(8,128)(2,1)}, bf16[1,2,4,64,512]{4,3,2,1,0:T(8,128)(2,1)S(1)}, u32[]{:S(2)}) copy-start(bf16[1,2,4,64,512]{4,3,2,1,0:T(8,128)(2,1)S(1)} %collective-permute-done.10.refs_2_) | copy-start | bytes 1572868
  81.9 15.2 %collective-permute-start.27 = (bf16[200,512]{1,0:T(8,128)(2,1)S(1)}, bf16[200,512]{1,0:T(8,128)(2,1)S(1)}, u32[]{:S(2)}, u32[]{:S(2)}) collective-permute-start(bf16[200,512]{1,0:T(8,128)(2,1)S(1)} %collective-permute-done.25.refs_12_), channel_id=1, source_target_pairs={{0,1},{1,3},{3,2},{2,0},{4,5},{5,7},{7,6},{6,4},{8,9},{9,11},{11,1... | collective-permute-start | bytes 614408 | tf_op jit(solution)/shard_map/ppermute | solution.py:57
  87.0 14.5 %collective-permute-start.28 = (bf16[200,512]{1,0:T(8,128)(2,1)S(1)}, bf16[200,512]{1,0:T(8,128)(2,1)S(1)}, u32[]{:S(2)}, u32[]{:S(2)}) collective-permute-start(bf16[200,512]{1,0:T(8,128)(2,1)S(1)} %collective-permute-done.26.refs_13_), channel_id=1, source_target_pairs={{0,1},{1,3},{3,2},{2,0},{4,5},{5,7},{7,6},{6,4},{8,9},{9,11},{11,1... | collective-permute-start | bytes 614408 | tf_op jit(solution)/shard_map/ppermute | solution.py:57
  88.2 17.9 %collective-permute-start.20 = (bf16[208,512]{1,0:T(8,128)(2,1)S(1)}, bf16[208,512]{1,0:T(8,128)(2,1)S(1)}, u32[]{:S(2)}, u32[]{:S(2)}) collective-permute-start(bf16[208,512]{1,0:T(8,128)(2,1)S(1)} %collective-permute-done.18.refs_3_), channel_id=1, source_target_pairs={{0,1},{1,3},{3,2},{2,0},{4,5},{5,7},{7,6},{6,4},{8,9},{9,11},{11,1... | collective-permute-start | bytes 638984 | tf_op jit(solution)/shard_map/ppermute | solution.py:57
  92.8 15.6 %collective-permute-start.19 = (bf16[208,512]{1,0:T(8,128)(2,1)S(1)}, bf16[208,512]{1,0:T(8,128)(2,1)S(1)}, u32[]{:S(2)}, u32[]{:S(2)}) collective-permute-start(bf16[208,512]{1,0:T(8,128)(2,1)S(1)} %collective-permute-done.17.refs_2_), channel_id=1, source_target_pairs={{0,1},{1,3},{3,2},{2,0},{4,5},{5,7},{7,6},{6,4},{8,9},{9,11},{11,1... | collective-permute-start | bytes 638984 | tf_op jit(solution)/shard_map/ppermute | solution.py:57
  93.1 44.4 %collective-permute-start.13 = (bf16[1,2,4,64,512]{4,3,2,1,0:T(8,128)(2,1)S(1)}, bf16[1,2,4,64,512]{4,3,2,1,0:T(8,128)(2,1)}, u32[]{:S(2)}, u32[]{:S(2)}) collective-permute-start(bf16[1,2,4,64,512]{4,3,2,1,0:T(8,128)(2,1)S(1)} %maximum_bitcast_fusion.refs_1_), channel_id=1, source_target_pairs={{0,4},{4,0},{8,12},{12,8},{16,20},{20,16},{24,28},{28,24},{1,5},{5... | collective-permute-start | bytes 1572872 | tf_op jit(solution)/shard_map/ppermute | solution.py:47
  97.2 40.3 %collective-permute-start.14 = (bf16[1,2,4,64,512]{4,3,2,1,0:T(8,128)(2,1)S(1)}, bf16[1,2,4,64,512]{4,3,2,1,0:T(8,128)(2,1)}, u32[]{:S(2)}, u32[]{:S(2)}) collective-permute-start(bf16[1,2,4,64,512]{4,3,2,1,0:T(8,128)(2,1)S(1)} %collective-permute-done.10.refs_2_), channel_id=1, source_target_pairs={{0,4},{4,0},{8,12},{12,8},{16,20},{20,16},{24,28},{28,24},{1,5},{5... | collective-permute-start | bytes 1572872 | tf_op jit(solution)/shard_map/ppermute | solution.py:47
  101.6 36.0 %collective-permute-start.15 = (bf16[1,2,4,64,512]{4,3,2,1,0:T(8,128)(2,1)}, bf16[1,2,4,64,512]{4,3,2,1,0:T(8,128)(2,1)}, u32[]{:S(2)}, u32[]{:S(2)}) collective-permute-start(bf16[1,2,4,64,512]{4,3,2,1,0:T(8,128)(2,1)} %collective-permute-done.11.refs_3_), channel_id=1, source_target_pairs={{0,4},{4,0},{8,12},{12,8},{16,20},{20,16},{24,28},{28,24},{1,5},{5... | collective-permute-start | bytes 1572872 | tf_op jit(solution)/shard_map/ppermute | solution.py:47
  106.1 31.4 %collective-permute-start.16 = (bf16[1,2,4,64,512]{4,3,2,1,0:T(8,128)(2,1)}, bf16[1,2,4,64,512]{4,3,2,1,0:T(8,128)(2,1)}, u32[]{:S(2)}, u32[]{:S(2)}) collective-permute-start(bf16[1,2,4,64,512]{4,3,2,1,0:T(8,128)(2,1)} %collective-permute-done.12.refs_4_), channel_id=1, source_target_pairs={{0,4},{4,0},{8,12},{12,8},{16,20},{20,16},{24,28},{28,24},{1,5},{5... | collective-permute-start | bytes 1572872 | tf_op jit(solution)/shard_map/ppermute | solution.py:47
  108.4 6.7 %collective-permute-start.22 = (bf16[208,512]{1,0:T(8,128)(2,1)S(1)}, bf16[208,512]{1,0:T(8,128)(2,1)S(1)}, u32[]{:S(2)}, u32[]{:S(2)}) collective-permute-start(bf16[208,512]{1,0:T(8,128)(2,1)S(1)} %collective-permute-done.20.refs_5_), channel_id=1, source_target_pairs={{0,1},{1,3},{3,2},{2,0},{4,5},{5,7},{7,6},{6,4},{8,9},{9,11},{11,1... | collective-permute-start | bytes 638984 | tf_op jit(solution)/shard_map/ppermute | solution.py:57
  115.2 6.7 %collective-permute-start.21 = (bf16[208,512]{1,0:T(8,128)(2,1)S(1)}, bf16[208,512]{1,0:T(8,128)(2,1)S(1)}, u32[]{:S(2)}, u32[]{:S(2)}) collective-permute-start(bf16[208,512]{1,0:T(8,128)(2,1)S(1)} %collective-permute-done.19.refs_4_), channel_id=1, source_target_pairs={{0,1},{1,3},{3,2},{2,0},{4,5},{5,7},{7,6},{6,4},{8,9},{9,11},{11,1... | collective-permute-start | bytes 638984 | tf_op jit(solution)/shard_map/ppermute | solution.py:57
  172.1 7.6 %collective-permute-start.35 = (bf16[208,512]{1,0:T(8,128)(2,1)}, bf16[208,512]{1,0:T(8,128)(2,1)S(1)}, u32[]{:S(2)}, u32[]{:S(2)}) collective-permute-start(bf16[208,512]{1,0:T(8,128)(2,1)} %get-tuple-element.85), channel_id=1, source_target_pairs={{0,2},{1,0},{3,1},{2,3},{4,6},{5,4},{7,5},{6,7},{8,10},{9,8},{11,9... | collective-permute-start | bytes 638984 | tf_op jit(solution)/shard_map/ppermute | solution.py:57
  172.1 12.1 %collective-permute-start.29 = (bf16[208,512]{1,0:T(8,128)(2,1)}, bf16[208,512]{1,0:T(8,128)(2,1)S(1)}, u32[]{:S(2)}, u32[]{:S(2)}) collective-permute-start(bf16[208,512]{1,0:T(8,128)(2,1)} %get-tuple-element.77), channel_id=1, source_target_pairs={{0,2},{1,0},{3,1},{2,3},{4,6},{5,4},{7,5},{6,7},{8,10},{9,8},{11,9... | collective-permute-start | bytes 638984 | tf_op jit(solution)/shard_map/ppermute | solution.py:57
  180.7 8.2 %collective-permute-start.36 = (bf16[208,512]{1,0:T(8,128)(2,1)S(1)}, bf16[208,512]{1,0:T(8,128)(2,1)S(1)}, u32[]{:S(2)}, u32[]{:S(2)}) collective-permute-start(bf16[208,512]{1,0:T(8,128)(2,1)S(1)} %add_convert_fusion.11), channel_id=1, source_target_pairs={{0,2},{1,0},{3,1},{2,3},{4,6},{5,4},{7,5},{6,7},{8,10},{9,8},{11,9... | collective-permute-start | bytes 638984 | tf_op jit(solution)/shard_map/ppermute | solution.py:57
  185.2 8.2 %collective-permute-start.30 = (bf16[208,512]{1,0:T(8,128)(2,1)S(1)}, bf16[208,512]{1,0:T(8,128)(2,1)S(1)}, u32[]{:S(2)}, u32[]{:S(2)}) collective-permute-start(bf16[208,512]{1,0:T(8,128)(2,1)S(1)} %add_convert_fusion.13), channel_id=1, source_target_pairs={{0,2},{1,0},{3,1},{2,3},{4,6},{5,4},{7,5},{6,7},{8,10},{9,8},{11,9... | collective-permute-start | bytes 638984 | tf_op jit(solution)/shard_map/ppermute | solution.py:57
  189.9 6.6 %collective-permute-start.37 = (bf16[208,512]{1,0:T(8,128)(2,1)S(1)}, bf16[208,512]{1,0:T(8,128)(2,1)S(1)}, u32[]{:S(2)}, u32[]{:S(2)}) collective-permute-start(bf16[208,512]{1,0:T(8,128)(2,1)S(1)} %add_convert_fusion.10), channel_id=1, source_target_pairs={{0,2},{1,0},{3,1},{2,3},{4,6},{5,4},{7,5},{6,7},{8,10},{9,8},{11,9... | collective-permute-start | bytes 638984 | tf_op jit(solution)/shard_map/ppermute | solution.py:57
  194.4 9.2 %collective-permute-start.31 = (bf16[208,512]{1,0:T(8,128)(2,1)S(1)}, bf16[208,512]{1,0:T(8,128)(2,1)S(1)}, u32[]{:S(2)}, u32[]{:S(2)}) collective-permute-start(bf16[208,512]{1,0:T(8,128)(2,1)S(1)} %add_convert_fusion.12), channel_id=1, source_target_pairs={{0,2},{1,0},{3,1},{2,3},{4,6},{5,4},{7,5},{6,7},{8,10},{9,8},{11,9... | collective-permute-start | bytes 638984 | tf_op jit(solution)/shard_map/ppermute | solution.py:57
  211.8 1.6 collective-permute-start.38
  211.9 51.9 %collective-permute-start.52 = (bf16[4,2,4,64,512]{4,3,2,1,0:T(8,128)(2,1)}, bf16[4,2,4,64,512]{4,3,2,1,0:T(8,128)(2,1)S(1)}, u32[]{:S(2)}, u32[]{:S(2)}) collective-permute-start(bf16[4,2,4,64,512]{4,3,2,1,0:T(8,128)(2,1)} %get-tuple-element.122), channel_id=1, source_target_pairs={{0,4},{4,0},{8,12},{12,8},{16,20},{20,16},{24,28},{28,24},{1,5},{5... | collective-permute-start | bytes 6291464 | tf_op jit(solution)/shard_map/ppermute | solution.py:47
  212.4 14.4 %collective-permute-start.32 = (bf16[400,512]{1,0:T(8,128)(2,1)S(1)}, bf16[400,512]{1,0:T(8,128)(2,1)S(1)}, u32[]{:S(2)}, u32[]{:S(2)}) collective-permute-start(bf16[400,512]{1,0:T(8,128)(2,1)S(1)} %copy-done.38), channel_id=1, source_target_pairs={{0,2},{1,0},{3,1},{2,3},{4,6},{5,4},{7,5},{6,7},{8,10},{9,8},{11,9... | collective-permute-start | bytes 1228808 | tf_op jit(solution)/shard_map/ppermute | solution.py:57
  213.4 10.3 %collective-permute-start.39 = (bf16[40,512]{1,0:T(8,128)(2,1)S(1)}, bf16[40,512]{1,0:T(8,128)(2,1)S(1)}, u32[]{:S(2)}, u32[]{:S(2)}) collective-permute-start(bf16[40,512]{1,0:T(8,128)(2,1)S(1)} %add_convert_fusion.15), channel_id=1, source_target_pairs={{0,8},{4,12},{8,0},{12,4},{16,24},{20,28},{24,16},{28,20},{1,9},{5... | collective-permute-start | bytes 122888 | tf_op jit(solution)/shard_map/ppermute | solution.py:47
  214.3 9.5 %collective-permute-start.40 = (bf16[40,512]{1,0:T(8,128)(2,1)S(1)}, bf16[40,512]{1,0:T(8,128)(2,1)S(1)}, u32[]{:S(2)}, u32[]{:S(2)}) collective-permute-start(bf16[40,512]{1,0:T(8,128)(2,1)S(1)} %add_convert_fusion.15), channel_id=1, source_target_pairs={{0,16},{4,20},{8,24},{12,28},{16,0},{20,4},{24,8},{28,12},{1,17},{... | collective-permute-start | bytes 122888 | tf_op jit(solution)/shard_map/ppermute | solution.py:47
  215.6 8.3 %collective-permute-start.41 = (bf16[40,512]{1,0:T(8,128)(2,1)S(1)}, bf16[40,512]{1,0:T(8,128)(2,1)S(1)}, u32[]{:S(2)}, u32[]{:S(2)}) collective-permute-start(bf16[40,512]{1,0:T(8,128)(2,1)S(1)} %add_convert_fusion.15), channel_id=1, source_target_pairs={{0,24},{4,28},{8,16},{12,20},{16,8},{20,12},{24,0},{28,4},{1,25},{... | collective-permute-start | bytes 122888 | tf_op jit(solution)/shard_map/ppermute | solution.py:47
  223.8 21.6 %collective-permute-start.45 = (bf16[4,4,256,128]{3,2,1,0:T(8,128)(2,1)}, bf16[4,4,256,128]{3,2,1,0:T(8,128)(2,1)S(1)}, u32[]{:S(2)}, u32[]{:S(2)}) collective-permute-start(bf16[4,4,256,128]{3,2,1,0:T(8,128)(2,1)} %get-tuple-element.120), channel_id=1, source_target_pairs={{0,4},{4,0},{8,12},{12,8},{16,20},{20,16},{24,28},{28,24},{1,5},{5... | collective-permute-start | bytes 3145736 | tf_op jit(solution)/shard_map/ppermute | solution.py:47
  223.9 4.6 %collective-permute-start.42 = (bf16[40,512]{1,0:T(8,128)(2,1)S(1)}, bf16[40,512]{1,0:T(8,128)(2,1)S(1)}, u32[]{:S(2)}, u32[]{:S(2)}) collective-permute-start(bf16[40,512]{1,0:T(8,128)(2,1)S(1)} %add_convert_fusion.14), channel_id=1, source_target_pairs={{0,1},{1,0},{2,3},{3,2},{4,5},{5,4},{6,7},{7,6},{8,9},{9,8},{10,11... | collective-permute-start | bytes 122888 | tf_op jit(solution)/shard_map/ppermute | solution.py:47
  225.0 5.9 %collective-permute-start.43 = (bf16[40,512]{1,0:T(8,128)(2,1)S(1)}, bf16[40,512]{1,0:T(8,128)(2,1)S(1)}, u32[]{:S(2)}, u32[]{:S(2)}) collective-permute-start(bf16[40,512]{1,0:T(8,128)(2,1)S(1)} %add_convert_fusion.14), channel_id=1, source_target_pairs={{0,2},{1,3},{2,0},{3,1},{4,6},{5,7},{6,4},{7,5},{8,10},{9,11},{10,... | collective-permute-start | bytes 122888 | tf_op jit(solution)/shard_map/ppermute | solution.py:47
  226.8 6.3 %collective-permute-start.44 = (bf16[40,512]{1,0:T(8,128)(2,1)S(1)}, bf16[40,512]{1,0:T(8,128)(2,1)S(1)}, u32[]{:S(2)}, u32[]{:S(2)}) collective-permute-start(bf16[40,512]{1,0:T(8,128)(2,1)S(1)} %add_convert_fusion.14), channel_id=1, source_target_pairs={{0,3},{1,2},{2,1},{3,0},{4,7},{5,6},{6,5},{7,4},{8,11},{9,10},{10,... | collective-permute-start | bytes 122888 | tf_op jit(solution)/shard_map/ppermute | solution.py:47
  228.5 12.0 %collective-permute-start.33 = (bf16[400,512]{1,0:T(8,128)(2,1)S(1)}, bf16[400,512]{1,0:T(8,128)(2,1)S(1)}, u32[]{:S(2)}, u32[]{:S(2)}) collective-permute-start(bf16[400,512]{1,0:T(8,128)(2,1)S(1)} %add_convert_fusion.5), channel_id=1, source_target_pairs={{0,2},{1,0},{3,1},{2,3},{4,6},{5,4},{7,5},{6,7},{8,10},{9,8},{11,9... | collective-permute-start | bytes 1228808 | tf_op jit(solution)/shard_map/ppermute | solution.py:57
  240.6 11.0 %collective-permute-start.34 = (bf16[400,512]{1,0:T(8,128)(2,1)S(1)}, bf16[400,512]{1,0:T(8,128)(2,1)S(1)}, u32[]{:S(2)}, u32[]{:S(2)}) collective-permute-start(bf16[400,512]{1,0:T(8,128)(2,1)S(1)} %add_convert_fusion.4), channel_id=1, source_target_pairs={{0,2},{1,0},{3,1},{2,3},{4,6},{5,4},{7,5},{6,7},{8,10},{9,8},{11,9... | collective-permute-start | bytes 1228808 | tf_op jit(solution)/shard_map/ppermute | solution.py:57
  245.6 8.3 %collective-permute-start.46 = (bf16[4,256,128]{2,1,0:T(8,128)(2,1)S(1)}, bf16[4,256,128]{2,1,0:T(8,128)(2,1)S(1)}, u32[]{:S(2)}, u32[]{:S(2)}) collective-permute-start(bf16[4,256,128]{2,1,0:T(8,128)(2,1)S(1)} %get-tuple-element.126), channel_id=1, source_target_pairs={{0,8},{4,12},{8,0},{12,4},{16,24},{20,28},{24,16},{28,20},{1,9},{5... | collective-permute-start | bytes 786440 | tf_op jit(solution)/shard_map/ppermute | solution.py:47
  246.5 10.9 %collective-permute-start.47 = (bf16[4,256,128]{2,1,0:T(8,128)(2,1)S(1)}, bf16[4,256,128]{2,1,0:T(8,128)(2,1)S(1)}, u32[]{:S(2)}, u32[]{:S(2)}) collective-permute-start(bf16[4,256,128]{2,1,0:T(8,128)(2,1)S(1)} %get-tuple-element.128), channel_id=1, source_target_pairs={{0,16},{4,20},{8,24},{12,28},{16,0},{20,4},{24,8},{28,12},{1,17},{... | collective-permute-start | bytes 786440 | tf_op jit(solution)/shard_map/ppermute | solution.py:47
  247.7 11.4 %collective-permute-start.48 = (bf16[4,256,128]{2,1,0:T(8,128)(2,1)S(1)}, bf16[4,256,128]{2,1,0:T(8,128)(2,1)S(1)}, u32[]{:S(2)}, u32[]{:S(2)}) collective-permute-start(bf16[4,256,128]{2,1,0:T(8,128)(2,1)S(1)} %get-tuple-element.127), channel_id=1, source_target_pairs={{0,24},{4,28},{8,16},{12,20},{16,8},{20,12},{24,0},{28,4},{1,25},{... | collective-permute-start | bytes 786440 | tf_op jit(solution)/shard_map/ppermute | solution.py:47
  259.4 7.4 %collective-permute-start.49 = (bf16[256,128]{1,0:T(8,128)(2,1)S(1)}, bf16[256,128]{1,0:T(8,128)(2,1)S(1)}, u32[]{:S(2)}, u32[]{:S(2)}) collective-permute-start(bf16[256,128]{1,0:T(8,128)(2,1)S(1)} %get-tuple-element.133), channel_id=1, source_target_pairs={{0,1},{1,0},{2,3},{3,2},{4,5},{5,4},{6,7},{7,6},{8,9},{9,8},{10,11... | collective-permute-start | bytes 196616 | tf_op jit(solution)/shard_map/ppermute | solution.py:47
  259.4 9.4 %collective-permute-start.50 = (bf16[256,128]{1,0:T(8,128)(2,1)S(1)}, bf16[256,128]{1,0:T(8,128)(2,1)S(1)}, u32[]{:S(2)}, u32[]{:S(2)}) collective-permute-start(bf16[256,128]{1,0:T(8,128)(2,1)S(1)} %get-tuple-element.135), channel_id=1, source_target_pairs={{0,2},{1,3},{2,0},{3,1},{4,6},{5,7},{6,4},{7,5},{8,10},{9,11},{10,... | collective-permute-start | bytes 196616 | tf_op jit(solution)/shard_map/ppermute | solution.py:47
  261.8 7.1 %collective-permute-start.51 = (bf16[256,128]{1,0:T(8,128)(2,1)S(1)}, bf16[256,128]{1,0:T(8,128)(2,1)S(1)}, u32[]{:S(2)}, u32[]{:S(2)}) collective-permute-start(bf16[256,128]{1,0:T(8,128)(2,1)S(1)} %get-tuple-element.134), channel_id=1, source_target_pairs={{0,3},{1,2},{2,1},{3,0},{4,7},{5,6},{6,5},{7,4},{8,11},{9,10},{10,... | collective-permute-start | bytes 196616 | tf_op jit(solution)/shard_map/ppermute | solution.py:47
  264.4 14.9 %collective-permute-start.53 = (bf16[2,4,64,512]{3,2,1,0:T(8,128)(2,1)S(1)}, bf16[2,4,64,512]{3,2,1,0:T(8,128)(2,1)S(1)}, u32[]{:S(2)}, u32[]{:S(2)}) collective-permute-start(bf16[2,4,64,512]{3,2,1,0:T(8,128)(2,1)S(1)} %get-tuple-element.123), channel_id=1, source_target_pairs={{0,8},{4,12},{8,0},{12,4},{16,24},{20,28},{24,16},{28,20},{1,9},{5... | collective-permute-start | bytes 1572872 | tf_op jit(solution)/shard_map/ppermute | solution.py:47
  265.0 22.8 %collective-permute-start.54 = (bf16[2,4,64,512]{3,2,1,0:T(8,128)(2,1)S(1)}, bf16[2,4,64,512]{3,2,1,0:T(8,128)(2,1)S(1)}, u32[]{:S(2)}, u32[]{:S(2)}) collective-permute-start(bf16[2,4,64,512]{3,2,1,0:T(8,128)(2,1)S(1)} %get-tuple-element.125), channel_id=1, source_target_pairs={{0,16},{4,20},{8,24},{12,28},{16,0},{20,4},{24,8},{28,12},{1,17},{... | collective-permute-start | bytes 1572872 | tf_op jit(solution)/shard_map/ppermute | solution.py:47
  266.8 21.1 %collective-permute-start.55 = (bf16[2,4,64,512]{3,2,1,0:T(8,128)(2,1)S(1)}, bf16[2,4,64,512]{3,2,1,0:T(8,128)(2,1)S(1)}, u32[]{:S(2)}, u32[]{:S(2)}) collective-permute-start(bf16[2,4,64,512]{3,2,1,0:T(8,128)(2,1)S(1)} %get-tuple-element.124), channel_id=1, source_target_pairs={{0,24},{4,28},{8,16},{12,20},{16,8},{20,12},{24,0},{28,4},{1,25},{... | collective-permute-start | bytes 1572872 | tf_op jit(solution)/shard_map/ppermute | solution.py:47
  (31 other events, 547.0 us)
